TPU v7x, 512 devices: a whole 4x8x8 slice. The times are simulated.
512 devices in a mesh: half: 2 (over core), blk: 64 (over z, y), sub: 4 (over x).
Axes of the slice: x: 4, y: 8, z: 8, core: 2. Of those that a mesh axis runs over, the one named last changes fastest.
Arguments:
- leaf_expansions: float32 [262144, 128], P(('half', 'blk', 'sub')), may hold values from -0.3 to 0.3
- leaf_occupied: int32 [262144], P(('half', 'blk', 'sub')), may hold values 0 or 1
- cone_angles: float32 [2, 768], replicated, may hold values from -3.140625 to 3.140625
- cone_need3: int32 [768, 512], P(('half', 'blk'), 'sub'), may hold values 0 or 1
- cone_need4: int32 [768, 64], P(('half', 'blk'), 'sub'), may hold values 0 or 1
Outputs:
- lowfreq: float32 [4096, 128], P(('half', 'blk', 'sub'))
- cone_expansions: float32 [768, 64, 128], P(('half', 'blk'), 'sub')
All inputs are finite; a program needn't handle non-finite values. No bound on the sum of `leaf_occupied` or of `cone_need3` or of `cone_need4` on one device may be relied on, other than what follows from the above.
Results may differ from a plain program's by a relative error of at most 0.00007.
Values sent between devices are 32-bit elements; how exact they have to be, the bound alone decides.
No kernel may reach another device: no remote copies, remote signals or barrier semaphores. Data moves between devices by JAX's collectives and lax.ppermute only.
A program may use at most 64 MiB of HBM per device.

v0:
```python
import math

import jax
import jax.numpy as jnp
from jax import lax
from jax.sharding import PartitionSpec as P

ORDER = 4


near_scale = 1.5
far_scale = 3.0
highest = lax.Precision.HIGHEST


def in_blocks(array, dim, peers):
    before, after = (array.shape[:dim], array.shape[dim + 1 :])
    return jnp.moveaxis(array.reshape(*before, peers, -1, *after), dim, 0)


def summed_on_arrival(array, axis, dim):
    parts = in_blocks(array, dim, lax.axis_size(axis))
    arrived = lax.all_to_all(parts, axis, split_axis=0, concat_axis=0, tiled=True)
    return arrived.sum(axis=0)


def chebyshev_points(per_axis):
    index = jnp.arange(per_axis, dtype=jnp.float32)
    return jnp.cos((2.0 * index + 1.0) * math.pi / (2.0 * per_axis))


def octant_signs():
    octant = jnp.arange(8, dtype=jnp.int32)
    bits = jnp.stack([octant // 4 % 2, octant // 2 % 2, octant % 2], -1)
    return bits.astype(jnp.float32) * 2.0 - 1.0


def octant_table(per_axis):
    points = chebyshev_points(per_axis)
    degree = jnp.arange(1, per_axis, dtype=jnp.float32)
    sign_pair = jnp.array([-1.0, 1.0], dtype=jnp.float32)
    shifted = (points[None, :] + sign_pair[:, None]) / 2.0
    poly_here = jnp.cos(degree[None, :] * jnp.arccos(points)[:, None])
    poly_there = jnp.cos(degree[None, None, :] * jnp.arccos(shifted)[:, :, None])
    single = 1.0 / per_axis + 2.0 / per_axis * jnp.einsum(
        "mk,bnk->bmn", poly_here, poly_there, precision=highest
    )
    signs = octant_signs()
    along_x = jnp.where((signs[:, 0] > 0)[:, None, None], single[1][None], single[0][None])
    along_y = jnp.where((signs[:, 1] > 0)[:, None, None], single[1][None], single[0][None])
    along_z = jnp.where((signs[:, 2] > 0)[:, None, None], single[1][None], single[0][None])
    full = jnp.einsum("oad,obe,ocf->odefabc", along_x, along_y, along_z, precision=highest)
    node_count = per_axis**3
    return full.reshape(8, node_count, node_count)


def node_offsets(per_axis):
    points = chebyshev_points(per_axis)
    index = jnp.arange(per_axis**3, dtype=jnp.int32)
    coords = jnp.stack(
        [
            points[index // (per_axis * per_axis)],
            points[index // per_axis % per_axis],
            points[index % per_axis],
        ],
        -1,
    )
    return coords[None, :, :] + octant_signs()[:, None, :]


def phases(angles, strength, per_axis):
    polar = angles[0]
    azimuth = angles[1]
    direction = jnp.stack(
        [jnp.sin(polar) * jnp.cos(azimuth), jnp.sin(polar) * jnp.sin(azimuth), jnp.cos(polar)], -1
    )
    offsets = node_offsets(per_axis)
    argument = offsets[None, :, :, 0] * direction[:, None, None, 0]
    argument = argument + offsets[None, :, :, 1] * direction[:, None, None, 1]
    argument = argument + offsets[None, :, :, 2] * direction[:, None, None, 2]
    argument = -strength * argument
    return (jnp.cos(argument), jnp.sin(argument))


def block_count(length, target):
    number = 1
    while length % (2 * number) == 0 and length // (2 * number) >= target:
        number = number * 2
    return number


def cone_products(box_data, cosines, sine_part, transfer):
    real_part = box_data[:, :, 0, :]
    imag_part = box_data[:, :, 1, :]
    mod_real = cosines[:, None] * real_part[None] - sine_part[:, None] * imag_part[None]
    mod_imag = cosines[:, None] * imag_part[None] + sine_part[:, None] * real_part[None]
    out_real = jnp.einsum("cbon,onm->cbm", mod_real, transfer, precision=highest)
    out_imag = jnp.einsum("cbon,onm->cbm", mod_imag, transfer, precision=highest)
    return jnp.concatenate([out_real, out_imag], -1)


def local(leaf_expansions, leaf_occupied, cone_angles, cone_need3, cone_need4):
    width = leaf_expansions.shape[1]
    node_count = width // 2
    subs = lax.axis_size("sub")
    groups = lax.axis_size("half") * lax.axis_size("blk")
    cone_local = cone_need3.shape[0]
    transfer = octant_table(ORDER)
    masked = leaf_expansions * leaf_occupied.astype(jnp.float32)[:, None]
    level_one_count = masked.shape[0] // 8
    pair_count = level_one_count // 2
    per_sub = pair_count // subs
    per_box = per_sub // 8
    masked = masked.reshape(level_one_count, 8, 2, node_count)
    level_one = jnp.einsum("poan,onm->pam", masked, transfer, precision=highest)
    level_one = level_one.reshape(pair_count, 2, 2, node_count)
    own = lax.dynamic_slice_in_dim(transfer, 2 * lax.axis_index("sub"), 2, 0)
    lowfreq = summed_on_arrival(
        jnp.einsum("kran,rnm->kam", level_one, own, precision=highest).reshape(
            per_sub * lax.axis_size("sub"), width
        ),
        "sub",
        0,
    )
    own_angles = lax.dynamic_slice_in_dim(
        cone_angles, lax.axis_index(("half", "blk")) * cone_local, cone_local, 1
    )
    cos_near, sin_near = phases(cone_angles, near_scale, ORDER)
    cone_total = cos_near.shape[0]
    blocks = block_count(cone_total, 128)
    block_size = cone_total // blocks
    box_data = lowfreq.reshape(per_box, 8, 2, node_count)

    def one_block(inputs):
        return cone_products(box_data, inputs[0], inputs[1], transfer)

    stacked = lax.map(
        one_block,
        (
            cos_near.reshape(blocks, block_size, 8, node_count),
            sin_near.reshape(blocks, block_size, 8, node_count),
        ),
    )
    level_three = stacked.reshape(cone_total, per_box, width)
    received = lax.all_to_all(level_three, ("half", "blk"), split_axis=0, concat_axis=1, tiled=True)
    received = received * cone_need3.astype(jnp.float32)[:, :, None]
    received = received.reshape(cone_local, groups // 8, 8, per_box, 2, node_count)
    cos_far, sin_far = phases(own_angles, far_scale, ORDER)
    real_part = received[:, :, :, :, 0, :]
    imag_part = received[:, :, :, :, 1, :]
    cos_wide = cos_far[:, None, :, None, :]
    sin_wide = sin_far[:, None, :, None, :]
    mod_real = cos_wide * real_part - sin_wide * imag_part
    mod_imag = cos_wide * imag_part + sin_wide * real_part
    four_real = jnp.einsum("cqotn,onm->cqtm", mod_real, transfer, precision=highest)
    four_imag = jnp.einsum("cqotn,onm->cqtm", mod_imag, transfer, precision=highest)
    joined = jnp.concatenate([four_real, four_imag], -1).reshape(cone_local, -1, width)
    cone_expansions = joined * cone_need4.astype(jnp.float32)[:, :, None]
    return (lowfreq, cone_expansions)


def solution(mesh):
    return jax.shard_map(
        local,
        mesh=mesh,
        in_specs=(
            P(("half", "blk", "sub"), None),
            P(("half", "blk", "sub")),
            P(),
            P(("half", "blk"), "sub"),
            P(("half", "blk"), "sub"),
        ),
        out_specs=(P(("half", "blk", "sub"), None), P(("half", "blk"), "sub", None)),
        check_vma=False,
    )
```

profile of v0, /device:TPU:1, one launch (start us, length us, event | category | flops | bytes accessed | tf_op | source)
XLA Modules:
  0.0 90.6 jit_solution(17780247378322274859)
XLA Ops:
  0.9 0.8 sqrt_atan2_fusion
  1.6 0.3 fusion.19
  2.1 0.5 broadcast_multiply_fusion.1
  2.6 0.6 copy.92
  3.2 0.1 broadcast_multiply_fusion.3
  3.4 0.3 reshape.561
  3.7 0.8 convolution_bitcast_fusion.2
  4.5 0.2 convolution_bitcast_fusion.5
  4.8 0.7 reshape_reshape.3
  5.5 4.8 %all-to-all-start = ((f32[4,8,128]{2,1,0:T(8,128)}), f32[4,8,128]{2,1,0:T(8,128)S(1)}, u32[]{:S(2)}, u32[]{:S(2)}) async-start(f32[4,8,128]{2,1,0:T(8,128)} %reshape_reshape.3), calls=%async_computation | async-start | bytes 32768 | tf_op jit(solution)/shard_map/all_to_all | solution.py:23
  10.3 0.6 fusion.47
  10.9 2.5 %compare_select_fusion.9 = (f32[64,1]{0,1:T(1,128)S(1)}, f32[64,1]{0,1:T(1,128)S(1)}) fusion(f32[]{:T(128)} %bitcast.18, f32[]{:T(128)} %bitcast.19, f32[]{:T(128)} %bitcast.21, f32[]{:T(128)} %bitcast.20), kind=kLoop, calls=%fused_computation.85 | loop fusion | flops 2624 | bytes 528 | tf_op jit(solution)/shard_map/gather | solution.py:64
  13.4 2.5 %compare_select_fusion.15 = f32[64,1]{0,1:T(1,128)S(1)} fusion(f32[]{:T(128)} %bitcast.18, f32[]{:T(128)} %bitcast.19, f32[]{:T(128)} %bitcast.21, f32[]{:T(128)} %bitcast.20), kind=kLoop, calls=%fused_computation.91 | loop fusion | flops 1088 | bytes 272 | tf_op jit(solution)/shard_map/gather | solution.py:62
  16.0 0.2 multiply_reduce_fusion.1
  16.4 9.3 %fusion.16 = (f32[4,192,8,64]{1,3,2,0:T(8,128)}, f32[4,192,8,64]{1,3,2,0:T(8,128)}) fusion(f32[4,192]{1,0:T(4,128)S(1)} %cos.83, f32[8,64]{1,0:T(8,128)S(1)} %get-tuple-element.123, f32[4,192]{1,0:T(4,128)S(1)} %mul.407, f32[8,64]{1,0:T(8,128)S(1)} %get-tuple-element.124, f32[4,192]{1,0:T(4,128)S(1)} %mul.402, f32[8,64]{1,0:T(8,128)S(1)} %get-tuple-element.122), kind=kLoop, calls=%fused_computation.25 | loop fusion | flops 2359296 | bytes 3161088 | tf_op jit(solution)/shard_map/sin | solution.py:82
  25.8 0.5 copy-done.1
  26.3 24.0 %while.11 = (s32[]{:T(128)}, f32[4,192,1,128]{3,1,0,2:T(8,128)}, f32[4,192,8,64]{1,3,2,0:T(8,128)}, f32[1,8,2,64]{3,1,2,0:T(8,128)S(1)}, f32[4,192,8,64]{1,3,2,0...) while((s32[]{:T(128)}, f32[4,192,1,128]{3,1,0,2:T(8,128)}, ...), condition=%wide.region_2.3_spmd.clone, body=%wide.region_1.2_spmd.clone.sunk | while | flops 151642112 | bytes 3467349 | solution.py:137
  26.3 0.5 broadcast_multiply_fusion.6
  26.8 1.2 %copy.124 = f32[8,64,64]{1,2,0:T(8,128)S(1)} copy(f32[8,64,64]{0,2,1:T(8,128)S(1)} %bitcast.139) | data formatting | bytes 262144 | tf_op jit(solution)/shard_map/reshape | solution.py:54
  28.0 1.8 %convolution_bitcast_fusion.9 = f32[192,1,64]{0,2,1:T(8,128)S(1)} fusion(f32[8,64,64]{1,2,0:T(8,128)S(1)} %copy.124, f32[4,192,8,64]{1,3,2,0:T(8,128)} %get-tuple-element.211, s32[]{:T(128)} %get-tuple-element.199, f32[4,192,8,64]{1,3,2,0:T(8,128)} %get-tuple-element.209, f32[8,64]{1,0:T(8,128)S(1)} %get-tuple-element.189, ...), kind=kOutput, calls=%fused_computation.2.clone.1 | convolution fusion | flops 75792384 | bytes 1233408 | tf_op jit(solution)/shard_map/while/body/eval_jaxpr/cbon,onm->cbm/dot_general | solution.py:97
  29.8 1.8 %convolution_bitcast_fusion.8 = f32[192,1,64]{0,2,1:T(8,128)S(1)} fusion(f32[8,64,64]{1,2,0:T(8,128)S(1)} %copy.124, f32[4,192,8,64]{1,3,2,0:T(8,128)} %get-tuple-element.211, s32[]{:T(128)} %get-tuple-element.199, f32[4,192,8,64]{1,3,2,0:T(8,128)} %get-tuple-element.209, f32[8,64]{1,0:T(8,128)S(1)} %get-tuple-element.189, ...), kind=kOutput, calls=%fused_computation.1.clone.1 | convolution fusion | flops 75792384 | bytes 1233408 | tf_op jit(solution)/shard_map/while/body/eval_jaxpr/cbon,onm->cbm/dot_general | solution.py:98
  31.6 0.1 copy.125
  31.7 0.6 constant_dynamic-update-slice_fusion.2
  32.3 0.5 broadcast_multiply_fusion.6
  32.8 1.2 %copy.124 = f32[8,64,64]{1,2,0:T(8,128)S(1)} copy(f32[8,64,64]{0,2,1:T(8,128)S(1)} %bitcast.139) | data formatting | bytes 262144 | tf_op jit(solution)/shard_map/reshape | solution.py:54
  34.0 1.8 %convolution_bitcast_fusion.9 = f32[192,1,64]{0,2,1:T(8,128)S(1)} fusion(f32[8,64,64]{1,2,0:T(8,128)S(1)} %copy.124, f32[4,192,8,64]{1,3,2,0:T(8,128)} %get-tuple-element.211, s32[]{:T(128)} %get-tuple-element.199, f32[4,192,8,64]{1,3,2,0:T(8,128)} %get-tuple-element.209, f32[8,64]{1,0:T(8,128)S(1)} %get-tuple-element.189, ...), kind=kOutput, calls=%fused_computation.2.clone.1 | convolution fusion | flops 75792384 | bytes 1233408 | tf_op jit(solution)/shard_map/while/body/eval_jaxpr/cbon,onm->cbm/dot_general | solution.py:97
  35.8 1.8 %convolution_bitcast_fusion.8 = f32[192,1,64]{0,2,1:T(8,128)S(1)} fusion(f32[8,64,64]{1,2,0:T(8,128)S(1)} %copy.124, f32[4,192,8,64]{1,3,2,0:T(8,128)} %get-tuple-element.211, s32[]{:T(128)} %get-tuple-element.199, f32[4,192,8,64]{1,3,2,0:T(8,128)} %get-tuple-element.209, f32[8,64]{1,0:T(8,128)S(1)} %get-tuple-element.189, ...), kind=kOutput, calls=%fused_computation.1.clone.1 | convolution fusion | flops 75792384 | bytes 1233408 | tf_op jit(solution)/shard_map/while/body/eval_jaxpr/cbon,onm->cbm/dot_general | solution.py:98
  37.7 0.6 constant_dynamic-update-slice_fusion.2
  38.3 0.5 broadcast_multiply_fusion.6
  38.8 1.2 %copy.124 = f32[8,64,64]{1,2,0:T(8,128)S(1)} copy(f32[8,64,64]{0,2,1:T(8,128)S(1)} %bitcast.139) | data formatting | bytes 262144 | tf_op jit(solution)/shard_map/reshape | solution.py:54
  40.0 1.8 %convolution_bitcast_fusion.9 = f32[192,1,64]{0,2,1:T(8,128)S(1)} fusion(f32[8,64,64]{1,2,0:T(8,128)S(1)} %copy.124, f32[4,192,8,64]{1,3,2,0:T(8,128)} %get-tuple-element.211, s32[]{:T(128)} %get-tuple-element.199, f32[4,192,8,64]{1,3,2,0:T(8,128)} %get-tuple-element.209, f32[8,64]{1,0:T(8,128)S(1)} %get-tuple-element.189, ...), kind=kOutput, calls=%fused_computation.2.clone.1 | convolution fusion | flops 75792384 | bytes 1233408 | tf_op jit(solution)/shard_map/while/body/eval_jaxpr/cbon,onm->cbm/dot_general | solution.py:97
  41.8 1.8 %convolution_bitcast_fusion.8 = f32[192,1,64]{0,2,1:T(8,128)S(1)} fusion(f32[8,64,64]{1,2,0:T(8,128)S(1)} %copy.124, f32[4,192,8,64]{1,3,2,0:T(8,128)} %get-tuple-element.211, s32[]{:T(128)} %get-tuple-element.199, f32[4,192,8,64]{1,3,2,0:T(8,128)} %get-tuple-element.209, f32[8,64]{1,0:T(8,128)S(1)} %get-tuple-element.189, ...), kind=kOutput, calls=%fused_computation.1.clone.1 | convolution fusion | flops 75792384 | bytes 1233408 | tf_op jit(solution)/shard_map/while/body/eval_jaxpr/cbon,onm->cbm/dot_general | solution.py:98
  43.7 0.7 constant_dynamic-update-slice_fusion.2
  44.3 0.5 broadcast_multiply_fusion.6
  44.8 1.2 %copy.124 = f32[8,64,64]{1,2,0:T(8,128)S(1)} copy(f32[8,64,64]{0,2,1:T(8,128)S(1)} %bitcast.139) | data formatting | bytes 262144 | tf_op jit(solution)/shard_map/reshape | solution.py:54
  46.0 1.8 %convolution_bitcast_fusion.9 = f32[192,1,64]{0,2,1:T(8,128)S(1)} fusion(f32[8,64,64]{1,2,0:T(8,128)S(1)} %copy.124, f32[4,192,8,64]{1,3,2,0:T(8,128)} %get-tuple-element.211, s32[]{:T(128)} %get-tuple-element.199, f32[4,192,8,64]{1,3,2,0:T(8,128)} %get-tuple-element.209, f32[8,64]{1,0:T(8,128)S(1)} %get-tuple-element.189, ...), kind=kOutput, calls=%fused_computation.2.clone.1 | convolution fusion | flops 75792384 | bytes 1233408 | tf_op jit(solution)/shard_map/while/body/eval_jaxpr/cbon,onm->cbm/dot_general | solution.py:97
  47.8 1.8 %convolution_bitcast_fusion.8 = f32[192,1,64]{0,2,1:T(8,128)S(1)} fusion(f32[8,64,64]{1,2,0:T(8,128)S(1)} %copy.124, f32[4,192,8,64]{1,3,2,0:T(8,128)} %get-tuple-element.211, s32[]{:T(128)} %get-tuple-element.199, f32[4,192,8,64]{1,3,2,0:T(8,128)} %get-tuple-element.209, f32[8,64]{1,0:T(8,128)S(1)} %get-tuple-element.189, ...), kind=kOutput, calls=%fused_computation.1.clone.1 | convolution fusion | flops 75792384 | bytes 1233408 | tf_op jit(solution)/shard_map/while/body/eval_jaxpr/cbon,onm->cbm/dot_general | solution.py:98
  49.7 0.6 constant_dynamic-update-slice_fusion.2
  50.3 18.2 %all-to-all-start.1 = ((f32[768,1,128]{2,1,0:T(1,128)}), f32[768,1,128]{2,1,0:T(1,128)S(1)}, u32[]{:S(2)}, u32[]{:S(2)}) async-start(f32[768,1,128]{2,1,0:T(1,128)} %bitcast.29), calls=%async_computation.1 | async-start | bytes 786432 | tf_op jit(solution)/shard_map/all_to_all | solution.py:145
  68.8 0.2 fusion.30
  69.0 17.6 %all-to-all-done.1 = f32[768,1,128]{2,1,0:T(1,128)S(1)} async-done(((f32[768,1,128]{2,1,0:T(1,128)}), f32[768,1,128]{2,1,0:T(1,128)S(1)}, u32[]{:S(2)}, u32[]{:S(2)}) %all-to-all-start.1) | async-done | bytes 393248 | tf_op jit(solution)/shard_map/all_to_all | solution.py:145
  86.6 0.5 all_to_all.20
  87.1 1.0 %broadcast_multiply_fusion.2 = f32[6,16,8,1,2,64]{5,4,2,1,0,3:T(2,128)S(1)} fusion(f32[6,16,8,1,2,64]{5,4,2,1,0,3:T(2,128)S(1)} %all_to_all.20, f32[6,16,8]{2,1,0:T(8,128)S(1)} %mul.415), kind=kLoop, calls=%fused_computation.40 | loop fusion | flops 98304 | bytes 789504 | tf_op jit(solution)/shard_map/mul | solution.py:146
  88.1 0.7 fusion.46
  88.7 0.1 multiply_subtract_fusion
  88.8 0.5 convolution_bitcast_fusion.4
  89.4 0.5 convolution_bitcast_fusion.3
  89.9 0.7 fusion.28
  (51 shorter events, 1.4 us)
Async XLA Ops:
  2.0 1.2 %copy-start.5 = (s32[512]{0:T(512)S(1)}, s32[512]{0:T(512)}, u32[]{:S(2)}) copy-start(s32[512]{0:T(512)} %param.9) | copy-start | bytes 6148
  2.1 1.2 %copy-start = (f32[512,128]{1,0:T(8,128)S(1)}, f32[512,128]{1,0:T(8,128)}, u32[]{:S(2)}) copy-start(f32[512,128]{1,0:T(8,128)} %param.8) | copy-start | bytes 786436
  2.6 13.4 %copy-start.2 = (f32[2,768]{1,0:T(2,128)S(1)}, f32[2,768]{1,0:T(2,128)}, u32[]{:S(2)}) copy-start(f32[2,768]{1,0:T(2,128)} %param.10) | copy-start | bytes 18436
  5.5 20.2 %all-to-all-start = ((f32[4,8,128]{2,1,0:T(8,128)}), f32[4,8,128]{2,1,0:T(8,128)S(1)}, u32[]{:S(2)}, u32[]{:S(2)}) async-start(f32[4,8,128]{2,1,0:T(8,128)} %reshape_reshape.3), calls=%async_computation | async-start | bytes 32768 | tf_op jit(solution)/shard_map/all_to_all | solution.py:23
  25.7 0.6 copy-start.1
  25.8 42.7 %copy-start.3 = (s32[6,128]{1,0:T(8,128)S(1)}, s32[6,128]{1,0:T(8,128)}, u32[]{:S(2)}) copy-start(s32[6,128]{1,0:T(8,128)} %param.11) | copy-start | bytes 9220
  25.8 42.9 %copy-start.4 = (s32[6,16]{1,0:T(8,128)S(1)}, s32[6,16]{1,0:T(8,128)}, u32[]{:S(2)}) copy-start(s32[6,16]{1,0:T(8,128)} %param.12) | copy-start | bytes 1156
  50.3 36.2 %all-to-all-start.1 = ((f32[768,1,128]{2,1,0:T(1,128)}), f32[768,1,128]{2,1,0:T(1,128)S(1)}, u32[]{:S(2)}, u32[]{:S(2)}) async-start(f32[768,1,128]{2,1,0:T(1,128)} %bitcast.29), calls=%async_computation.1 | async-start | bytes 786432 | tf_op jit(solution)/shard_map/all_to_all | solution.py:145
where the time goes:
time: 91.3 us; the launch traced here: 90.6 us
  starting transfers between devices  23 us (25%)
  other arithmetic  20.3 us (22%)
  waiting for transfers between devices  17.6 us (19%)
  matrix products  16.4 us (18%)
  local copies, waits for them, and re-layouts  12.1 us (13%)
  between operations  0.92 us (1%)
    all_to_all x1, starting transfers between devices, local(): lax.all_to_all(level_three, ('half', 'blk'), split_axis=0, concat_axis=1,...  18.2 us
    all_to_all x1, waiting for transfers between devices, local(): lax.all_to_all(level_three, ('half', 'blk'), split_axis=0, concat_axis=1,...  17.6 us
    sin x1, other arithmetic, phases(): return (jnp.cos(argument), jnp.sin(argument))  9.27 us
    dot_general x4, matrix products, cone_products(): jnp.einsum('cbon,onm->cbm', mod_real, transfer, precision=highest)  7.04 us
    dot_general x4, matrix products, cone_products(): jnp.einsum('cbon,onm->cbm', mod_imag, transfer, precision=highest)  7.04 us
    reshape x5, local copies, waits for them, and re-layouts, octant_table(): return full.reshape(8, node_count, node_count)  5.36 us
    all_to_all x1, starting transfers between devices, summed_on_arrival(): lax.all_to_all(parts, axis, split_axis=0, concat_axis=0, tiled=True)  4.84 us
    dynamic_update_slice x8, local copies, waits for them, and re-layouts, local(): lax.map(one_block, (cos_near.reshape(blocks, block_size, 8, node_count),...  2.94 us
  transfers between devices with their start and end apart: 2, of which 1 were waited for; matrix products, arithmetic and copies ran while one was open for 17% of the time, Pallas kernels for 0%

commit v1 on v0

v1 whole, which is shorter than its diff:
```python
import math

import jax
import jax.numpy as jnp
import numpy as np
from jax import lax
from jax.experimental import pallas as pl
from jax.experimental.pallas import tpu as pltpu
from jax.sharding import Mesh
from jax.sharding import PartitionSpec as P

ORDER = 4
NODES = ORDER**3
OCTANTS = 8
WIDTH = 2 * NODES
NEAR = 1.5
f32 = jnp.float32
bf16 = jnp.bfloat16


def points():
    index = np.arange(ORDER, dtype=np.float64)
    return np.cos((2.0 * index + 1.0) * math.pi / (2.0 * ORDER))


def transfer_parts():
    here = points()
    degree = np.arange(1, ORDER)
    single = []
    for sign in (-1.0, 1.0):
        there = (here + sign) / 2.0
        poly_here = np.cos(degree[None, :] * np.arccos(here)[:, None])
        poly_there = np.cos(degree[None, :] * np.arccos(there)[:, None])
        single.append(1.0 / ORDER + 2.0 / ORDER * poly_there @ poly_here.T)
    rows = []
    for octant in range(OCTANTS):
        along = [single[octant // 4 % 2], single[octant // 2 % 2], single[octant % 2]]
        full = np.kron(np.kron(along[0], along[1]), along[2])
        rows.append(np.kron(np.eye(2), full))
    table = np.concatenate(rows).astype(np.float32)
    high = table.astype(bf16)
    low = (table - high.astype(np.float32)).astype(bf16)
    return np.concatenate([high, low], 1)


def lane_points():
    here = points()
    index = np.arange(NODES)
    coords = np.stack([here[index // ORDER**2], here[index // ORDER % ORDER], here[index % ORDER]])
    coords = NEAR * np.concatenate([coords, -coords], 1)
    sign = np.concatenate([np.ones(NODES), -np.ones(NODES)])[None]
    pad = np.zeros((4, WIDTH))
    return np.concatenate([coords, sign, pad]).astype(np.float32)


def split(value):
    high = value.astype(bf16)
    low = (value - high.astype(f32)).astype(bf16)
    return high, low


def joined(product, rows):
    top = product[:rows]
    bottom = product[rows:]
    return top[:, :WIDTH] + (top[:, WIDTH:] + bottom[:, :WIDTH]) + bottom[:, WIDTH:]


def times(value, weights):
    high, low = split(value)
    product = jnp.dot(jnp.concatenate([high, low]), weights, preferred_element_type=f32)
    return joined(product, value.shape[0])


def leaf_kernel(place, occupied, leaves, weights, out, masked, first):
    rows = leaves.shape[0]
    for block in range(rows // 128):
        line = occupied[block : block + 1, :].astype(f32)
        column = jnp.transpose(jnp.broadcast_to(line, (128, 128)))
        masked[pl.ds(128 * block, 128), :] = leaves[pl.ds(128 * block, 128), :] * column
    boxes = rows // OCTANTS
    parts = [masked[pl.ds(o, boxes, stride=OCTANTS), :] for o in range(OCTANTS)]
    first[...] = times(jnp.concatenate(parts, 1), weights[...])
    pairs = [first[pl.ds(r, boxes // 2, stride=2), :] for r in range(2)]
    start = pl.multiple_of(place[0] * (2 * WIDTH), 2 * WIDTH)
    own = weights[pl.ds(start, 2 * WIDTH), :]
    second = times(jnp.concatenate(pairs, 1), own)
    chunks = second.reshape(out.shape[1:])
    for copy in range(out.shape[0]):
        out[copy] = chunks


def phase_kernel(place, angles, lanes, cosines, sines):
    cones = cosines.shape[0]
    total = angles.shape[1]
    mine = OCTANTS * (cones // 16) // OCTANTS
    row = lax.broadcasted_iota(jnp.int32, (cones, total), 0)
    col = lax.broadcasted_iota(jnp.int32, (cones, total), 1)
    group = row // mine
    wanted = (group * OCTANTS + place[0]) * mine + (row - group * mine)
    pick = (col == wanted).astype(f32)
    chosen = lax.dot_general(
        pick,
        angles[...],
        (((1,), (1,)), ((), ())),
        precision=lax.Precision.HIGHEST,
        preferred_element_type=f32,
    )
    sin_a = jnp.sin(chosen)
    cos_a = jnp.cos(chosen)
    direct = [
        sin_a[:, 0:1] * cos_a[:, 1:2],
        sin_a[:, 0:1] * sin_a[:, 1:2],
        cos_a[:, 0:1],
    ]
    argument = direct[0] * lanes[0:1, :] + direct[1] * lanes[1:2, :] + direct[2] * lanes[2:3, :]
    base = (jnp.cos(argument), jnp.sin(argument))
    steps = []
    for d in range(3):
        angle = jnp.broadcast_to(direct[d] * NEAR, (cones, WIDTH)) * lanes[3:4, :]
        steps.append((jnp.cos(angle), jnp.sin(angle)))

    def turned(value, step, sign):
        c, s = value
        a, b = step
        if sign > 0:
            return (c * a - s * b, s * a + c * b)
        return (c * a + s * b, s * a - c * b)

    for octant in range(OCTANTS):
        bits = (octant // 4 % 2, octant // 2 % 2, octant % 2)
        value = base
        for d in range(3):
            value = turned(value, steps[d], 2 * bits[d] - 1)
        cosines[:, octant * WIDTH : (octant + 1) * WIDTH] = value[0]
        sines[:, octant * WIDTH : (octant + 1) * WIDTH] = value[1]


def level_kernel(place, received, cosines, sines, need, weights, out, lowfreq, operand, mask):
    cones = cosines.shape[0]
    groups = need.shape[0]
    mine = cones // groups
    subs = received.shape[0] // OCTANTS
    low_own = received[subs * place[0]]
    for s in range(1, subs):
        low_own = low_own + received[subs * place[0] + s]
    lowfreq[...] = low_own
    for g in range(groups):
        mask[pl.ds(g * mine, mine), :] = need[g, :mine, :]
    for y in range(OCTANTS):
        box = received[subs * y]
        for s in range(1, subs):
            box = box + received[subs * y + s]
        turned = pltpu.roll(box, NODES, 1)
        for o in range(OCTANTS):
            at = pl.ds(o * WIDTH, WIDTH)
            value = cosines[:, at] * box[o : o + 1, :] + sines[:, at] * turned[o : o + 1, :]
            high, low = split(value)
            operand[pl.ds(2 * cones * y, cones), at] = high
            operand[pl.ds(2 * cones * y + cones, cones), at] = low
    product = jnp.dot(operand[...], weights[...], preferred_element_type=f32)
    shift = lax.rem(2 * WIDTH - place[1] * OCTANTS, WIDTH)
    needed = pltpu.roll(mask[...], shift, 1)
    parts = []
    for y in range(OCTANTS):
        at = pl.ds(y * WIDTH, WIDTH)
        three = joined(product[2 * cones * y : 2 * cones * (y + 1)], cones)
        three = three * needed[:, y : y + 1]
        c = cosines[:, at]
        s = sines[:, at]
        parts.append((c * c - s * s) * three + (2.0 * c * s) * pltpu.roll(three, NODES, 1))
    four = times(jnp.concatenate(parts, 1), weights[...])
    for g in range(groups):
        out[g, :mine, :] = four[g * mine : (g + 1) * mine]


def vmem():
    return pl.BlockSpec(memory_space=pltpu.VMEM)


def smem():
    return pl.BlockSpec(memory_space=pltpu.SMEM)


def local(leaf_expansions, leaf_occupied, cone_angles, cone_need3, cone_need4):
    rows, width = leaf_expansions.shape
    cone_local = cone_need3.shape[0]
    subs = lax.axis_size("sub")
    eights = lax.axis_size("y")
    groups = lax.axis_size("half") * lax.axis_size("z")
    cones = groups * cone_local
    weights = jnp.asarray(transfer_parts())
    lanes = jnp.asarray(lane_points())
    y_place = lax.axis_index("y")
    group_place = lax.axis_index(("half", "z"))
    partial = pl.pallas_call(
        leaf_kernel,
        out_shape=jax.ShapeDtypeStruct((eights, subs, 8, width), f32),
        in_specs=[smem(), vmem(), vmem(), vmem()],
        out_specs=vmem(),
        scratch_shapes=[pltpu.VMEM((rows, width), f32), pltpu.VMEM((rows // 8, width), f32)],
        name="leaves",
    )(
        lax.axis_index("sub").reshape(1),
        leaf_occupied.reshape(rows // 128, 128),
        leaf_expansions,
        weights,
    )
    received = lax.all_to_all(
        partial.reshape(eights * subs, 8, width),
        ("y", "sub"),
        split_axis=0,
        concat_axis=0,
        tiled=True,
    )
    need = jnp.pad(cone_need3.astype(f32), ((0, 8 - cone_local), (0, 0)))
    need = lax.all_to_all(
        jnp.broadcast_to(need[None], (groups, 8, need.shape[1])),
        ("half", "z"),
        split_axis=0,
        concat_axis=0,
        tiled=True,
    )
    cosines, sines = pl.pallas_call(
        phase_kernel,
        out_shape=[jax.ShapeDtypeStruct((cones, OCTANTS * width), f32)] * 2,
        in_specs=[smem(), vmem(), vmem()],
        out_specs=[vmem(), vmem()],
        name="phases",
    )(y_place.reshape(1), cone_angles, lanes)
    four, lowfreq = pl.pallas_call(
        level_kernel,
        out_shape=[
            jax.ShapeDtypeStruct((groups, 8, width), f32),
            jax.ShapeDtypeStruct((8, width), f32),
        ],
        in_specs=[smem()] + [vmem()] * 5,
        out_specs=[vmem(), vmem()],
        scratch_shapes=[
            pltpu.VMEM((2 * cones * OCTANTS, OCTANTS * width), bf16),
            pltpu.VMEM((cones, width), f32),
        ],
        name="levels",
    )(jnp.stack([y_place, group_place]), received, cosines, sines, need, weights)
    four = lax.all_to_all(four, ("half", "z"), split_axis=0, concat_axis=0, tiled=True)
    four = jnp.transpose(four[:, :cone_local, :], (1, 0, 2))
    return (lowfreq, four * cone_need4.astype(f32)[:, :, None])


def solution(mesh):
    halves, blocks, subs = mesh.devices.shape
    fine = Mesh(
        mesh.devices.reshape(halves, blocks // OCTANTS, OCTANTS, subs), ("half", "z", "y", "sub")
    )
    blk = ("half", "z", "y")
    return jax.shard_map(
        local,
        mesh=fine,
        in_specs=(
            P(blk + ("sub",), None),
            P(blk + ("sub",)),
            P(),
            P(blk, "sub"),
            P(blk, "sub"),
        ),
        out_specs=(P(blk + ("sub",), None), P(blk, "sub", None)),
        check_vma=False,
    )
```

time: 91.3 us -> 59.5 us (0.65)
  other arithmetic: 20.3 us -> 1.38 us
  matrix products: 16.4 us -> 0 us
  local copies, waits for them, and re-layouts: 12.1 us -> 2.64 us
  Pallas kernels: 0 us -> 9.27 us
  starting transfers between devices: 23 us -> 27.3 us
    dot_general x13 -> x0, matrix products: 16.4 us -> none  [the longest x4 7.04 us: cone_products(): jnp.einsum('cbon,onm->cbm', mod_real, transfer, precision=highest)]
    sin x1 -> x0, other arithmetic: 9.27 us -> none  [phases(): return (jnp.cos(argument), jnp.sin(argument))]
    pallas_call x0 -> x3, Pallas kernels: none -> 9.27 us  [the longest x1 4.01 us: local(): pl.pallas_call(level_kernel, out_shape=[jax.ShapeDtypeStruct((groups, 8,...]
    reshape x7 -> x0, local copies, waits for them, and re-layouts: 5.76 us -> none  [the longest x5 5.36 us: octant_table(): return full.reshape(8, node_count, node_count)]
    gather x2 -> x0, other arithmetic: 4.94 us -> none  [the longest x1 2.47 us: node_offsets(): points[index % per_axis]]
    all_to_all x2 -> x3, starting transfers between devices: 23 us -> 27.3 us  [the longest x1 11.8 us: local(): lax.all_to_all(jnp.broadcast_to(need[None], (groups, 8, need.shape[1])),...]
    dynamic_update_slice x8 -> x0, local copies, waits for them, and re-layouts: 2.94 us -> none  [local(): lax.map(one_block, (cos_near.reshape(blocks, block_size, 8, node_count),...]
    dot_general x6 -> x0, other arithmetic: 2.58 us -> none  [octant_table(): jnp.einsum('oad,obe,ocf->odefabc', along_x, along_y, along_z, precision=h...]
  transfers between devices with their start and end apart: 2 -> 3, of which waited for: 1 -> 3; matrix products, arithmetic and copies ran while one was open for 17% -> 1% of each run, Pallas kernels for 0% -> 9%
where the time goes in v1:
time: 59.5 us; the launch traced here: 59 us
  starting transfers between devices  27.3 us (46%)
  waiting for transfers between devices  17.7 us (30%)
  Pallas kernels  9.27 us (16%)
  local copies, waits for them, and re-layouts  2.64 us (4%)
  other arithmetic  1.38 us (2%)
  between operations  0.67 us (1%)
    all_to_all x1, starting transfers between devices, local(): lax.all_to_all(jnp.broadcast_to(need[None], (groups, 8, need.shape[1])),...  11.8 us
    all_to_all x1, starting transfers between devices, local(): lax.all_to_all(partial.reshape(eights * subs, 8, width), ('y', 'sub'), sp...  9.67 us
    all_to_all x1, waiting for transfers between devices, local(): lax.all_to_all(four, ('half', 'z'), split_axis=0, concat_axis=0, tiled=True)  7.07 us
    all_to_all x1, starting transfers between devices, local(): lax.all_to_all(four, ('half', 'z'), split_axis=0, concat_axis=0, tiled=True)  5.83 us
    all_to_all x1, waiting for transfers between devices, local(): lax.all_to_all(partial.reshape(eights * subs, 8, width), ('y', 'sub'), sp...  5.76 us
    all_to_all x1, waiting for transfers between devices, local(): lax.all_to_all(jnp.broadcast_to(need[None], (groups, 8, need.shape[1])),...  4.87 us
    pallas_call x1, Pallas kernels, local(): pl.pallas_call(level_kernel, out_shape=[jax.ShapeDtypeStruct((groups, 8,...  4.01 us
    pallas_call x1, Pallas kernels, local(): pl.pallas_call(phase_kernel, out_shape=[jax.ShapeDtypeStruct((cones, OCTA...  2.97 us
  transfers between devices with their start and end apart: 3, of which 3 were waited for; matrix products, arithmetic and copies ran while one was open for 1% of the time, Pallas kernels for 9%

profile of v1, /device:TPU:1, one launch (start us, length us, event | category | flops | bytes accessed | tf_op | source)
XLA Modules:
  0.0 59.0 jit_solution(5104153754462664891)
XLA Ops:
  0.6 0.7 %convert_element_type.8 = f32[6,128]{1,0:T(8,128)S(1)} convert(s32[6,128]{1,0:T(8,128)} %param.10) | non-fusion elementwise | flops 768 | bytes 6144 | tf_op jit(solution)/shard_map/convert_element_type | solution.py:215
  1.3 0.6 %broadcast_in_dim.2 = f32[16,8,128]{2,1,0:T(8,128)} broadcast(f32[8,128]{1,0:T(8,128)S(1)} %pad.4), dimensions={1,2} | broadcast | bytes 69632 | tf_op jit(solution)/shard_map/broadcast_in_dim | solution.py:217
  2.0 11.8 %all-to-all-start.1 = ((f32[16,8,128]{2,1,0:T(8,128)}), f32[16,8,128]{2,1,0:T(8,128)S(1)}, u32[]{:S(2)}, u32[]{:S(2)}) async-start(f32[16,8,128]{2,1,0:T(8,128)} %broadcast_in_dim.2), calls=%async_computation.1 | async-start | bytes 131072 | tf_op jit(solution)/shard_map/all_to_all | solution.py:216
  13.8 2.3 %leaves.2 = f32[8,4,8,128]{3,2,1,0:T(8,128)} custom-call(s32[1]{0:T(128)} %bitcast.2.place, s32[4,128]{1,0:T(4,128)} %bitcast.10, f32[512,128]{1,0:T(8,128)} %leaves.3, bf16[1024,256]{1,0:T(8,128)(2,1)} %constant.28.clone.weights), custom_call_target="tpu_custom_call" | custom-call | tf_op jit(solution)/shard_map/leaves/pallas_call | solution.py:195
  16.1 4.9 %all-to-all-done.1.need = f32[16,8,128]{2,1,0:T(8,128)S(1)} async-done(((f32[16,8,128]{2,1,0:T(8,128)}), f32[16,8,128]{2,1,0:T(8,128)S(1)}, u32[]{:S(2)}, u32[]{:S(2)}) %all-to-all-start.1) | async-done | bytes 65568 | tf_op jit(solution)/shard_map/all_to_all | solution.py:216
  21.0 0.0 copy-start.1
  21.0 0.6 %copy-done.1 = f32[16,8,128]{2,1,0:T(8,128)} copy-done((f32[16,8,128]{2,1,0:T(8,128)}, f32[16,8,128]{2,1,0:T(8,128)S(1)}, u32[]{:S(2)}) %copy-start.1) | copy-done | bytes 65560
  21.6 9.7 %all-to-all-start = ((f32[32,8,128]{2,1,0:T(8,128)}), f32[32,8,128]{2,1,0:T(8,128)S(1)}, u32[]{:S(2)}, u32[]{:S(2)}) async-start(f32[32,8,128]{2,1,0:T(8,128)} %bitcast.9), calls=%async_computation | async-start | bytes 262144 | tf_op jit(solution)/shard_map/all_to_all | solution.py:208
  31.3 3.0 %phases.1 = (f32[96,1024]{1,0:T(8,128)}, f32[96,1024]{1,0:T(8,128)}) custom-call(s32[1]{0:T(128)} %bitcast.place, f32[2,768]{1,0:T(2,128)} %angles.1, f32[8,128]{1,0:T(8,128)} %constant.29.clone.lanes), custom_call_target="tpu_custom_call" | custom-call | tf_op jit(solution)/shard_map/phases/pallas_call | solution.py:223
  34.2 0.6 %pad_add_fusion.place = s32[2]{0:T(128)} fusion(s32[1]{0:T(128)} %bitcast.1, s32[1]{0:T(128)} %bitcast.place), kind=kLoop, calls=%fused_computation.2 | loop fusion | flops 2 | bytes 16 | tf_op jit(solution)/shard_map/stack | solution.py:243
  34.8 5.8 %all-to-all-done.received = f32[32,8,128]{2,1,0:T(8,128)S(1)} async-done(((f32[32,8,128]{2,1,0:T(8,128)}), f32[32,8,128]{2,1,0:T(8,128)S(1)}, u32[]{:S(2)}, u32[]{:S(2)}) %all-to-all-start) | async-done | bytes 131104 | tf_op jit(solution)/shard_map/all_to_all | solution.py:208
  40.6 0.0 copy-start
  40.6 0.7 %copy-done = f32[32,8,128]{2,1,0:T(8,128)} copy-done((f32[32,8,128]{2,1,0:T(8,128)}, f32[32,8,128]{2,1,0:T(8,128)S(1)}, u32[]{:S(2)}) %copy-start) | copy-done | bytes 131096
  41.3 4.0 %levels.1 = (f32[16,8,128]{2,1,0:T(8,128)}, f32[8,128]{1,0:T(8,128)}) custom-call(s32[2]{0:T(128)} %pad_add_fusion.place, f32[32,8,128]{2,1,0:T(8,128)} %copy-done, f32[96,1024]{1,0:T(8,128)} %get-tuple-element.6.cosines, f32[96,1024]{1,0:T(8,128)} %get-tuple-element.7.sines, f32[16,8,128]{2,1,0:T(8,128)} %copy-done.1, bf16[1024,256]{1,0:T(8,128)(2,1)} %constant.28.clone.weights), custom_call_target="tpu_custom_call" | custom-call | tf_op jit(solution)/shard_map/levels/pallas_call | solution.py:230
  45.3 0.0 copy-start.2
  45.3 5.8 %all-to-all-start.2 = ((f32[16,8,128]{2,1,0:T(8,128)}), f32[16,8,128]{2,1,0:T(8,128)S(1)}, u32[]{:S(2)}, u32[]{:S(2)}) async-start(f32[16,8,128]{2,1,0:T(8,128)} %get-tuple-element.9), calls=%async_computation.2 | async-start | bytes 131072 | tf_op jit(solution)/shard_map/all_to_all | solution.py:244
  51.1 0.0 copy-done.2
  51.1 0.1 copy.9
  51.2 7.1 %all-to-all-done.2 = f32[16,8,128]{2,1,0:T(8,128)S(1)} async-done(((f32[16,8,128]{2,1,0:T(8,128)}), f32[16,8,128]{2,1,0:T(8,128)S(1)}, u32[]{:S(2)}, u32[]{:S(2)}) %all-to-all-start.2) | async-done | bytes 65568 | tf_op jit(solution)/shard_map/all_to_all | solution.py:244
  58.3 0.1 fusion
  58.4 0.6 %copy.10 = f32[6,16,128]{2,1,0:T(8,128)} copy(f32[6,16,128]{2,0,1:T(8,128)S(1)} %fusion) | data formatting | bytes 98304
  (2 shorter events, 0.0 us)
Async XLA Ops:
  2.0 19.0 %all-to-all-start.1 = ((f32[16,8,128]{2,1,0:T(8,128)}), f32[16,8,128]{2,1,0:T(8,128)S(1)}, u32[]{:S(2)}, u32[]{:S(2)}) async-start(f32[16,8,128]{2,1,0:T(8,128)} %broadcast_in_dim.2), calls=%async_computation.1 | async-start | bytes 131072 | tf_op jit(solution)/shard_map/all_to_all | solution.py:216
  21.0 0.6 %copy-start.1 = (f32[16,8,128]{2,1,0:T(8,128)}, f32[16,8,128]{2,1,0:T(8,128)S(1)}, u32[]{:S(2)}) copy-start(f32[16,8,128]{2,1,0:T(8,128)S(1)} %all-to-all-done.1.need) | copy-start | bytes 196612
  21.6 19.0 %all-to-all-start = ((f32[32,8,128]{2,1,0:T(8,128)}), f32[32,8,128]{2,1,0:T(8,128)S(1)}, u32[]{:S(2)}, u32[]{:S(2)}) async-start(f32[32,8,128]{2,1,0:T(8,128)} %bitcast.9), calls=%async_computation | async-start | bytes 262144 | tf_op jit(solution)/shard_map/all_to_all | solution.py:208
  40.6 0.7 %copy-start = (f32[32,8,128]{2,1,0:T(8,128)}, f32[32,8,128]{2,1,0:T(8,128)S(1)}, u32[]{:S(2)}) copy-start(f32[32,8,128]{2,1,0:T(8,128)S(1)} %all-to-all-done.received) | copy-start | bytes 393220
  45.3 5.8 %copy-start.2 = (s32[6,16]{1,0:T(8,128)S(1)}, s32[6,16]{1,0:T(8,128)}, u32[]{:S(2)}) copy-start(s32[6,16]{1,0:T(8,128)} %param.11) | copy-start | bytes 1156
  45.3 13.0 %all-to-all-start.2 = ((f32[16,8,128]{2,1,0:T(8,128)}), f32[16,8,128]{2,1,0:T(8,128)S(1)}, u32[]{:S(2)}, u32[]{:S(2)}) async-start(f32[16,8,128]{2,1,0:T(8,128)} %get-tuple-element.9), calls=%async_computation.2 | async-start | bytes 131072 | tf_op jit(solution)/shard_map/all_to_all | solution.py:244

commit v2 on v1

v2 whole, which is shorter than its diff:
```python
import math

import jax
import jax.numpy as jnp
import numpy as np
from jax import lax
from jax.experimental import pallas as pl
from jax.experimental.pallas import tpu as pltpu
from jax.sharding import Mesh
from jax.sharding import PartitionSpec as P

ORDER = 4
NODES = ORDER**3
OCTANTS = 8
WIDTH = 2 * NODES
NEAR = 1.5
FAR = 3.0
f32 = jnp.float32
bf16 = jnp.bfloat16


def points():
    index = np.arange(ORDER, dtype=np.float64)
    return np.cos((2.0 * index + 1.0) * math.pi / (2.0 * ORDER))


def transfer_rows():
    here = points()
    degree = np.arange(1, ORDER)
    single = []
    for sign in (-1.0, 1.0):
        there = (here + sign) / 2.0
        poly_here = np.cos(degree[None, :] * np.arccos(here)[:, None])
        poly_there = np.cos(degree[None, :] * np.arccos(there)[:, None])
        single.append(1.0 / ORDER + 2.0 / ORDER * poly_there @ poly_here.T)
    rows, quarters = [], []
    for octant in range(OCTANTS):
        along = [single[octant // 4 % 2], single[octant // 2 % 2], single[octant % 2]]
        full = np.kron(np.kron(along[0], along[1]), along[2])
        rows.append(np.kron(np.eye(2), full))
        quarters.append(np.kron(np.ones((2, 2)), full))
    table = np.concatenate(rows).astype(np.float32)
    high = table.astype(bf16)
    low = (table - high.astype(np.float32)).astype(bf16)
    return np.concatenate([high, low], 1), np.concatenate(quarters).astype(np.float32)


def near_columns():
    here = points()
    index = np.arange(NODES)
    coords = np.stack([here[index // ORDER**2], here[index // ORDER % ORDER], here[index % ORDER]])
    return np.tile(NEAR * coords.reshape(-1, 1), (1, WIDTH)).astype(np.float32)


def octant_rows():
    here = points()
    index = np.arange(NODES)
    coords = np.stack([here[index // ORDER**2], here[index // ORDER % ORDER], here[index % ORDER]])
    coords = np.concatenate([coords, coords], 1)
    octant = np.arange(OCTANTS)
    signs = np.stack([octant // 4 % 2, octant // 2 % 2, octant % 2]) * 2.0 - 1.0
    near = np.tile(NEAR * signs[:, :, None], (1, 1, WIDTH))
    far = FAR * (coords[:, None, :] + signs[:, :, None])
    return np.concatenate([near, far]).astype(np.float32).reshape(-1, WIDTH)


def split(value):
    high = value.astype(bf16)
    low = (value - high.astype(f32)).astype(bf16)
    return high, low


def joined(product, rows):
    top = product[:rows]
    bottom = product[rows:]
    return top[:, :WIDTH] + (top[:, WIDTH:] + bottom[:, :WIDTH]) + bottom[:, WIDTH:]


def times(value, weights):
    high, low = split(value)
    product = jnp.dot(jnp.concatenate([high, low]), weights, preferred_element_type=f32)
    return joined(product, value.shape[0])


def leaf_kernel(place, occupied, leaves, weights, out, masked, first):
    rows = leaves.shape[0]
    for block in range(rows // 128):
        line = occupied[block : block + 1, :].astype(f32)
        column = jnp.transpose(jnp.broadcast_to(line, (128, 128)))
        masked[pl.ds(128 * block, 128), :] = leaves[pl.ds(128 * block, 128), :] * column
    boxes = rows // OCTANTS
    parts = [masked[pl.ds(o, boxes, stride=OCTANTS), :] for o in range(OCTANTS)]
    first[...] = times(jnp.concatenate(parts, 1), weights[...])
    pairs = [first[pl.ds(r, boxes // 2, stride=2), :] for r in range(2)]
    start = pl.multiple_of(place[0] * (2 * WIDTH), 2 * WIDTH)
    own = weights[pl.ds(start, 2 * WIDTH), :]
    second = times(jnp.concatenate(pairs, 1), own)
    out[...] = second.reshape(out.shape)


def cosine_sine(x):
    turns = jnp.floor(x * (2.0 / math.pi) + 0.5)
    r = x - turns * 1.5703125
    r = r - turns * 4.837512969970703125e-4
    r = r - turns * 7.54978995489188216e-8
    z = r * r
    sine = r + r * z * (-1.6666654611e-1 + z * (8.3321608736e-3 - z * 1.9515295891e-4))
    cosine = 4.166664568298827e-2 + z * (-1.388731625493765e-3 + z * 2.443315711809948e-5)
    cosine = 1.0 - 0.5 * z + z * z * cosine
    quarter = turns.astype(jnp.int32)
    swap = (quarter & 1) == 1
    c = jnp.where(swap, sine, cosine)
    s = jnp.where(swap, cosine, sine)
    return jnp.where(((quarter + 1) & 2) == 2, -c, c), jnp.where((quarter & 2) == 2, -s, s)


def column_of(rows):
    count, width = rows.shape
    flags = jnp.concatenate([rows, jnp.zeros((WIDTH - count, width), f32)])
    if width < WIDTH:
        flags = jnp.concatenate([flags, jnp.zeros((WIDTH, WIDTH - width), f32)], 1)
    turned = jnp.transpose(flags)
    return [jnp.broadcast_to(turned[:width, c : c + 1], (width, WIDTH)) for c in range(count)]


def table_kernel(
    place, angles, need_three, need_four, columns, octants, quarters, high, low, far_cos, far_sin, keep
):
    cones = need_three.shape[0]
    row = lax.broadcasted_iota(jnp.int32, (8, WIDTH), 0)
    polar = jnp.zeros((8, WIDTH), f32)
    azimuth = jnp.zeros((8, WIDTH), f32)
    for c in range(cones):
        polar = jnp.where(row == c, angles[0, place[0] * cones + c], polar)
        azimuth = jnp.where(row == c, angles[1, place[0] * cones + c], azimuth)
    cos_p, sin_p = cosine_sine(polar)
    cos_a, sin_a = cosine_sine(azimuth)
    direction = (sin_p * cos_a, sin_p * sin_a, cos_p)
    real = lax.broadcasted_iota(jnp.int32, (NODES, WIDTH), 1) < NODES
    three_flags = column_of(need_three[...].astype(f32))
    four_flags = column_of(need_four[...].astype(f32))
    boxes = need_four.shape[1]
    for c in range(cones):
        along = [direction[d][c : c + 1, :] for d in range(3)]

        def dot(table, start, size):
            value = along[0] * table[start : start + size, :]
            value = value + along[1] * table[start + size : start + 2 * size, :]
            return value + along[2] * table[start + 2 * size : start + 3 * size, :]

        c0, s0 = cosine_sine(dot(columns, 0, NODES))
        ways = (
            (jnp.where(real, c0, -s0), jnp.where(real, -s0, -c0)),
            (jnp.where(real, s0, c0), jnp.where(real, c0, -s0)),
        )
        c1, s1 = cosine_sine(dot(octants, 0, OCTANTS))
        for o in range(OCTANTS):
            for part in range(2):
                at = pl.ds(o * WIDTH + part * NODES, NODES)
                value = ways[part][0] * c1[o : o + 1, :] + ways[part][1] * s1[o : o + 1, :]
                top, rest = split(value * quarters[at, :])
                high[at, c * WIDTH : (c + 1) * WIDTH] = top
                low[at, c * WIDTH : (c + 1) * WIDTH] = rest
        c3, s3 = cosine_sine(dot(octants, 3 * OCTANTS, OCTANTS))
        s3 = jnp.where(real[:OCTANTS], s3, -s3)
        at = pl.ds(c * WIDTH, WIDTH)
        far_cos[at, :] = jnp.concatenate([c3] * boxes) * three_flags[c]
        far_sin[at, :] = jnp.concatenate([s3] * boxes) * three_flags[c]
        keep[pl.ds(c * boxes, boxes), :] = four_flags[c]


def level_kernel(gathered, high, low, far_cos, far_sin, keep, weights, out, turned):
    boxes = gathered.shape[0] // OCTANTS
    rows = keep.shape[0]
    parts = [gathered[pl.ds(o, boxes, stride=OCTANTS), :] for o in range(OCTANTS)]
    top, rest = split(jnp.concatenate(parts, 1))
    both = jnp.dot(jnp.concatenate([top, rest]), high[...], preferred_element_type=f32)
    three = both[:boxes] + (both[boxes:] + jnp.dot(top, low[...], preferred_element_type=f32))
    for c in range(three.shape[1] // WIDTH):
        at = pl.ds(c * boxes, boxes)
        value = three[:, c * WIDTH : (c + 1) * WIDTH]
        turned[at, :] = far_cos[at, :] * value + far_sin[at, :] * pltpu.roll(value, NODES, 1)
    parts = [turned[pl.ds(o, rows, stride=OCTANTS), :] for o in range(OCTANTS)]
    four = times(jnp.concatenate(parts, 1), weights[...])
    out[...] = (four * keep[...]).reshape(out.shape)


def vmem():
    return pl.BlockSpec(memory_space=pltpu.VMEM)


def smem():
    return pl.BlockSpec(memory_space=pltpu.SMEM)


def here(array):
    return pltpu.with_memory_space_constraint(array, pltpu.VMEM)


def local(leaf_expansions, leaf_occupied, cone_angles, cone_need3, cone_need4):
    rows, width = leaf_expansions.shape
    cones, boxes = cone_need3.shape
    fours = cone_need4.shape[1]
    subs = lax.axis_size("sub")
    blocks = lax.axis_size("z") * lax.axis_size("y")
    parts, quarters = transfer_rows()
    weights = jnp.asarray(parts)
    partial = pl.pallas_call(
        leaf_kernel,
        out_shape=jax.ShapeDtypeStruct((subs, 8, width), f32),
        in_specs=[smem(), vmem(), vmem(), vmem()],
        out_specs=vmem(),
        scratch_shapes=[pltpu.VMEM((rows, width), f32), pltpu.VMEM((rows // 8, width), f32)],
        compiler_params=pltpu.CompilerParams(vmem_limit_bytes=24 << 20),
        name="leaves",
    )(
        lax.axis_index("sub").reshape(1),
        leaf_occupied.reshape(rows // 128, 128),
        leaf_expansions,
        weights,
    )
    received = lax.all_to_all(partial, "sub", split_axis=0, concat_axis=0, tiled=True)
    tables = pl.pallas_call(
        table_kernel,
        out_shape=[
            pltpu.VMEM((OCTANTS * width, cones * width), bf16),
            pltpu.VMEM((OCTANTS * width, cones * width), bf16),
            pltpu.VMEM((cones * boxes, width), f32),
            pltpu.VMEM((cones * boxes, width), f32),
            pltpu.VMEM((cones * fours, width), f32),
        ],
        in_specs=[smem(), smem()] + [vmem()] * 5,
        out_specs=[vmem()] * 5,
        compiler_params=pltpu.CompilerParams(vmem_limit_bytes=24 << 20),
        name="tables",
    )(
        lax.axis_index(("half", "z", "y")).reshape(1),
        cone_angles,
        cone_need3,
        cone_need4,
        jnp.asarray(near_columns()),
        jnp.asarray(octant_rows()),
        jnp.asarray(quarters),
    )
    received, *tables = lax.optimization_barrier((received, *tables))
    lowfreq = received.sum(axis=0)
    gathered = lax.all_to_all(
        jnp.broadcast_to(lowfreq[None], (blocks, 8, width)),
        ("z", "y"),
        split_axis=0,
        concat_axis=0,
        tiled=True,
    )
    gathered = lax.all_gather(gathered.reshape(blocks * 8, width), "half", tiled=True)
    cone_expansions = pl.pallas_call(
        level_kernel,
        out_shape=jax.ShapeDtypeStruct((cones, fours, width), f32),
        in_specs=[vmem()] * 7,
        out_specs=vmem(),
        scratch_shapes=[pltpu.VMEM((cones * boxes, width), f32)],
        compiler_params=pltpu.CompilerParams(vmem_limit_bytes=24 << 20),
        name="levels",
    )(here(gathered), *[here(table) for table in tables], weights)
    return (lowfreq, cone_expansions)


def solution(mesh):
    halves, blocks, subs = mesh.devices.shape
    fine = Mesh(
        mesh.devices.reshape(halves, blocks // OCTANTS, OCTANTS, subs), ("half", "z", "y", "sub")
    )
    blk = ("half", "z", "y")
    return jax.shard_map(
        local,
        mesh=fine,
        in_specs=(
            P(blk + ("sub",), None),
            P(blk + ("sub",)),
            P(),
            P(blk, "sub"),
            P(blk, "sub"),
        ),
        out_specs=(P(blk + ("sub",), None), P(blk, "sub", None)),
        check_vma=False,
    )
```

time: 59.5 us -> 53.8 us (0.904)
  blocking collectives: 0 us -> 34 us
  starting transfers between devices: 27.3 us -> 4.84 us
  waiting for transfers between devices: 17.7 us -> 0.01 us
  local copies, waits for them, and re-layouts: 2.64 us -> 8.59 us
  Pallas kernels: 9.27 us -> 5.14 us
  other arithmetic: 1.38 us -> 0.01 us
    all_to_all x0 -> x1, blocking collectives: none -> 28.7 us  [local(): lax.all_to_all(jnp.broadcast_to(lowfreq[None], (blocks, 8, width)), ('z',...]
    all_to_all x3 -> x1, starting transfers between devices: 27.3 us -> 4.84 us  [local(): lax.all_to_all(partial, 'sub', split_axis=0, concat_axis=0, tiled=True)]
    all_to_all x3 -> x1, waiting for transfers between devices: 17.7 us -> 0.01 us  [local(): lax.all_to_all(partial, 'sub', split_axis=0, concat_axis=0, tiled=True)]
    unnamed x7 -> x26, local copies, waits for them, and re-layouts: 1.92 us -> 8.57 us
    all_gather x0 -> x1, blocking collectives: none -> 5.27 us  [local(): lax.all_gather(gathered.reshape(blocks * 8, width), 'half', tiled=True)]
    pallas_call x3, Pallas kernels: 9.27 us -> 5.14 us  [the longest x1 2.14 us: local(): pl.pallas_call(table_kernel, out_shape=[pltpu.VMEM((OCTANTS * width, cone...]
    convert_element_type x2 -> x0, other arithmetic: 0.69 us -> none  [the longest x1 0.69 us: local(): need = jnp.pad(cone_need3.astype(f32), ((0, 8 - cone_local), (0, 0)))]
    broadcast_in_dim x1, local copies, waits for them, and re-layouts: 0.63 us -> 0.02 us  [local(): jnp.broadcast_to(lowfreq[None], (blocks, 8, width))]
  transfers between devices with their start and end apart: 3 -> 1, of which waited for: 3 -> 0; matrix products, arithmetic and copies ran while one was open for 1% -> 0% of each run, Pallas kernels for 9% -> 4%
where the time goes in v2:
time: 53.8 us; the launch traced here: 53.2 us
  blocking collectives  34 us (63%)
  local copies, waits for them, and re-layouts  8.59 us (16%)
  Pallas kernels  5.14 us (10%)
  starting transfers between devices  4.84 us (9%)
  between operations  0.68 us (1%)
    all_to_all x1, blocking collectives, local(): lax.all_to_all(jnp.broadcast_to(lowfreq[None], (blocks, 8, width)), ('z',...  28.7 us
    unnamed x26, local copies, waits for them, and re-layouts  8.57 us
    all_gather x1, blocking collectives, local(): lax.all_gather(gathered.reshape(blocks * 8, width), 'half', tiled=True)  5.27 us
    all_to_all x1, starting transfers between devices, local(): lax.all_to_all(partial, 'sub', split_axis=0, concat_axis=0, tiled=True)  4.84 us
    pallas_call x1, Pallas kernels, local(): pl.pallas_call(table_kernel, out_shape=[pltpu.VMEM((OCTANTS * width, cone...  2.14 us
    pallas_call x1, Pallas kernels, local(): pl.pallas_call(level_kernel, out_shape=jax.ShapeDtypeStruct((cones, fours...  1.9 us
    pallas_call x1, Pallas kernels, local(): pl.pallas_call(leaf_kernel, out_shape=jax.ShapeDtypeStruct((subs, 8, widt...  1.09 us
  transfers between devices with their start and end apart: 1, of which 0 were waited for; matrix products, arithmetic and copies ran while one was open for 0% of the time, Pallas kernels for 4%

profile of v2, /device:TPU:1, one launch (start us, length us, event | category | flops | bytes accessed | tf_op | source)
XLA Modules:
  0.0 53.2 jit_solution(319523460615370435)
XLA Ops:
  0.6 0.0 copy-start
  0.6 1.0 %copy-done = bf16[1024,256]{1,0:T(8,128)(2,1)S(1)} copy-done((bf16[1024,256]{1,0:T(8,128)(2,1)S(1)}, bf16[1024,256]{1,0:T(8,128)(2,1)}, u32[]{:S(2)}) %copy-start) | copy-done | bytes 524312
  1.7 0.0 copy-start.5
  1.7 0.9 %copy-done.5 = f32[512,128]{1,0:T(8,128)S(1)} copy-done((f32[512,128]{1,0:T(8,128)S(1)}, f32[512,128]{1,0:T(8,128)}, u32[]{:S(2)}) %copy-start.5) | copy-done | bytes 262168
  2.6 0.0 copy-start.11
  2.6 0.7 %copy-done.11 = s32[512]{0:T(512)S(1)} copy-done((s32[512]{0:T(512)S(1)}, s32[512]{0:T(512)}, u32[]{:S(2)}) %copy-start.11) | copy-done | bytes 2072
  3.3 0.0 copy-start.1
  3.3 1.1 %leaves.2 = f32[4,8,128]{2,1,0:T(8,128)} custom-call(s32[1]{0:T(128)} %bitcast.place, s32[4,128]{1,0:T(4,128)S(1)} %bitcast.4, f32[512,128]{1,0:T(8,128)S(1)} %copy-done.5, bf16[1024,256]{1,0:T(8,128)(2,1)S(1)} %copy-done), custom_call_target="tpu_custom_call" | custom-call | tf_op jit(solution)/shard_map/leaves/pallas_call | solution.py:208
  4.4 4.8 %all-to-all-start = ((f32[4,8,128]{2,1,0:T(8,128)}), f32[4,8,128]{2,1,0:T(8,128)S(1)}, u32[]{:S(2)}, u32[]{:S(2)}) async-start(f32[4,8,128]{2,1,0:T(8,128)} %leaves.2), calls=%async_computation | async-start | bytes 32768 | tf_op jit(solution)/shard_map/all_to_all | solution.py:222
  9.3 0.0 copy-start.4
  9.3 1.0 %copy-done.4 = f32[1024,128]{1,0:T(8,128)S(1)} copy-done((f32[1024,128]{1,0:T(8,128)S(1)}, f32[1024,128]{1,0:T(8,128)}, u32[]{:S(2)}) %copy-start.4) | copy-done | bytes 524312
  10.3 0.0 copy-start.6
  10.3 0.9 %copy-done.6 = f32[192,128]{1,0:T(8,128)S(1)} copy-done((f32[192,128]{1,0:T(8,128)S(1)}, f32[192,128]{1,0:T(8,128)}, u32[]{:S(2)}) %copy-start.6) | copy-done | bytes 98328
  11.2 0.0 copy-start.7
  11.2 0.7 %copy-done.7 = f32[48,128]{1,0:T(8,128)S(1)} copy-done((f32[48,128]{1,0:T(8,128)S(1)}, f32[48,128]{1,0:T(8,128)}, u32[]{:S(2)}) %copy-start.7) | copy-done | bytes 24600
  11.9 0.0 copy-start.8
  11.9 0.7 %copy-done.8 = f32[2,768]{1,0:T(2,128)S(1)} copy-done((f32[2,768]{1,0:T(2,128)S(1)}, f32[2,768]{1,0:T(2,128)}, u32[]{:S(2)}) %copy-start.8) | copy-done | bytes 6168
  12.6 0.0 copy-start.9
  12.6 0.7 %copy-done.9 = s32[6,128]{1,0:T(8,128)S(1)} copy-done((s32[6,128]{1,0:T(8,128)S(1)}, s32[6,128]{1,0:T(8,128)}, u32[]{:S(2)}) %copy-start.9) | copy-done | bytes 3096
  13.3 0.0 copy-start.10
  13.3 0.7 %copy-done.10 = s32[6,16]{1,0:T(8,128)S(1)} copy-done((s32[6,16]{1,0:T(8,128)S(1)}, s32[6,16]{1,0:T(8,128)}, u32[]{:S(2)}) %copy-start.10) | copy-done | bytes 408
  14.0 2.1 %tables.1 = (bf16[1024,768]{1,0:T(8,128)(2,1)S(1)}, bf16[1024,768]{1,0:T(8,128)(2,1)S(1)}, f32[768,128]{1,0:T(8,128)S(1)}, f32[768,128]{1,0:T(8,128)S(1)}, f32[96,128]{1,0:T(8,128)S(1)}) custom-call(s32[1]{0:T(128)} %bitcast.2.place, f32[2,768]{1,0:T(2,128)S(1)} %copy-done.8, s32[6,128]{1,0:T(8,128)S(1)} %copy-done.9, s32[6,16]{1,0:T(8,128)S(1)} %copy-done.10, ...), custom_call_target="tpu_custom_call" | custom-call | tf_op jit(solution)/shard_map/tables/pallas_call | solution.py:223
  16.1 0.0 copy-start.2
  16.1 1.2 %copy-done.2 = bf16[1024,768]{1,0:T(8,128)(2,1)} copy-done((bf16[1024,768]{1,0:T(8,128)(2,1)}, bf16[1024,768]{1,0:T(8,128)(2,1)S(1)}, u32[]{:S(2)}) %copy-start.2) | copy-done | bytes 1572888
  17.3 0.0 all-to-all-done
  17.3 0.0 copy-start.12
  17.3 0.0 copy-start.3
  17.4 28.7 %all_to_all.10 = f32[64,8,128]{2,1,0:T(8,128)S(1)} all-to-all(f32[64,8,128]{2,1,0:T(8,128)S(1)} %broadcast_in_dim.2), channel_id=1, replica_groups=mesh['half'=2,'z'=8,'y'=8,'sub'=4] {'z','y'}, dimensions={0} | all-to-all | bytes 524288 | tf_op jit(solution)/shard_map/all_to_all | solution.py:247
  46.1 5.3 %all_gather.3.gathered = f32[1024,128]{1,0:T(8,128)S(1)} all-gather(f32[512,128]{1,0:T(8,128)S(1)} %bitcast.5), channel_id=1, replica_groups=mesh['half'=2,'z'=8,'y'=8,'sub'=4] {'half'}, dimensions={0}, use_global_device_ids=true | all-gather | bytes 786432 | tf_op jit(solution)/shard_map/all_gather | solution.py:254
  51.3 0.0 copy-done.1
  51.3 0.0 copy-done.3
  51.3 1.9 %levels.1 = f32[6,16,128]{2,1,0:T(8,128)} custom-call(f32[1024,128]{1,0:T(8,128)S(1)} %all_gather.3.gathered, bf16[1024,768]{1,0:T(8,128)(2,1)S(1)} %get-tuple-element.19.high, bf16[1024,768]{1,0:T(8,128)(2,1)S(1)} %copy-done.3, f32[768,128]{1,0:T(8,128)S(1)} %get-tuple-element.21.far_cos, f32[768,128]{1,0:T(8,128)S(1)} %get-tuple-element.22.far_sin, ...), custom_call_target="tpu_custom_call" | custom-call | tf_op jit(solution)/shard_map/levels/pallas_call | solution.py:255
  53.2 0.0 copy-done.12
  (2 shorter events, 0.0 us)
Async XLA Ops:
  0.6 1.0 %copy-start = (bf16[1024,256]{1,0:T(8,128)(2,1)S(1)}, bf16[1024,256]{1,0:T(8,128)(2,1)}, u32[]{:S(2)}) copy-start(bf16[1024,256]{1,0:T(8,128)(2,1)} %constant.33.clone.weights) | copy-start | bytes 1572868
  1.7 0.9 %copy-start.5 = (f32[512,128]{1,0:T(8,128)S(1)}, f32[512,128]{1,0:T(8,128)}, u32[]{:S(2)}) copy-start(f32[512,128]{1,0:T(8,128)} %leaves.3) | copy-start | bytes 786436
  2.6 0.7 %copy-start.11 = (s32[512]{0:T(512)S(1)}, s32[512]{0:T(512)}, u32[]{:S(2)}) copy-start(s32[512]{0:T(512)} %param.10) | copy-start | bytes 6148
  3.3 48.0 %copy-start.1 = (bf16[1024,256]{1,0:T(8,128)(2,1)S(1)}, bf16[1024,256]{1,0:T(8,128)(2,1)}, u32[]{:S(2)}) copy-start(bf16[1024,256]{1,0:T(8,128)(2,1)} %constant.33.clone.weights) | copy-start | bytes 1572868
  4.4 12.9 %all-to-all-start = ((f32[4,8,128]{2,1,0:T(8,128)}), f32[4,8,128]{2,1,0:T(8,128)S(1)}, u32[]{:S(2)}, u32[]{:S(2)}) async-start(f32[4,8,128]{2,1,0:T(8,128)} %leaves.2), calls=%async_computation | async-start | bytes 32768 | tf_op jit(solution)/shard_map/all_to_all | solution.py:222
  9.3 1.0 %copy-start.4 = (f32[1024,128]{1,0:T(8,128)S(1)}, f32[1024,128]{1,0:T(8,128)}, u32[]{:S(2)}) copy-start(f32[1024,128]{1,0:T(8,128)} %constant.36.clone.quarters) | copy-start | bytes 1572868
  10.3 0.9 %copy-start.6 = (f32[192,128]{1,0:T(8,128)S(1)}, f32[192,128]{1,0:T(8,128)}, u32[]{:S(2)}) copy-start(f32[192,128]{1,0:T(8,128)} %constant.34.clone.columns) | copy-start | bytes 294916
  11.2 0.7 %copy-start.7 = (f32[48,128]{1,0:T(8,128)S(1)}, f32[48,128]{1,0:T(8,128)}, u32[]{:S(2)}) copy-start(f32[48,128]{1,0:T(8,128)} %constant.35.clone.octants) | copy-start | bytes 73732
  11.9 0.7 %copy-start.8 = (f32[2,768]{1,0:T(2,128)S(1)}, f32[2,768]{1,0:T(2,128)}, u32[]{:S(2)}) copy-start(f32[2,768]{1,0:T(2,128)} %angles.1) | copy-start | bytes 18436
  12.6 0.7 %copy-start.9 = (s32[6,128]{1,0:T(8,128)S(1)}, s32[6,128]{1,0:T(8,128)}, u32[]{:S(2)}) copy-start(s32[6,128]{1,0:T(8,128)} %need_three.1) | copy-start | bytes 9220
  13.3 0.7 %copy-start.10 = (s32[6,16]{1,0:T(8,128)S(1)}, s32[6,16]{1,0:T(8,128)}, u32[]{:S(2)}) copy-start(s32[6,16]{1,0:T(8,128)} %need_four.1) | copy-start | bytes 1156
  16.1 1.2 %copy-start.2 = (bf16[1024,768]{1,0:T(8,128)(2,1)}, bf16[1024,768]{1,0:T(8,128)(2,1)S(1)}, u32[]{:S(2)}) copy-start(bf16[1024,768]{1,0:T(8,128)(2,1)S(1)} %get-tuple-element.20.low) | copy-start | bytes 4718596
  17.3 35.9 %copy-start.12 = (f32[8,128]{1,0:T(8,128)}, f32[8,128]{1,0:T(8,128)S(1)}, u32[]{:S(2)}) copy-start(f32[8,128]{1,0:T(8,128)S(1)} %reduce_sum.9) | copy-start | bytes 12292
  17.3 34.0 %copy-start.3 = (bf16[1024,768]{1,0:T(8,128)(2,1)S(1)}, bf16[1024,768]{1,0:T(8,128)(2,1)}, u32[]{:S(2)}) copy-start(bf16[1024,768]{1,0:T(8,128)(2,1)} %copy-done.2) | copy-start | bytes 4718596

commit v3 on v2

v3 whole, which is shorter than its diff:
```python
import math

import jax
import jax.numpy as jnp
import numpy as np
from jax import lax
from jax.experimental import pallas as pl
from jax.experimental.pallas import tpu as pltpu
from jax.sharding import Mesh
from jax.sharding import PartitionSpec as P

ORDER = 4
NODES = ORDER**3
OCTANTS = 8
WIDTH = 2 * NODES
NEAR = 1.5
FAR = 3.0
f32 = jnp.float32
bf16 = jnp.bfloat16


def points():
    index = np.arange(ORDER, dtype=np.float64)
    return np.cos((2.0 * index + 1.0) * math.pi / (2.0 * ORDER))


def transfer_rows():
    here = points()
    degree = np.arange(1, ORDER)
    single = []
    for sign in (-1.0, 1.0):
        there = (here + sign) / 2.0
        poly_here = np.cos(degree[None, :] * np.arccos(here)[:, None])
        poly_there = np.cos(degree[None, :] * np.arccos(there)[:, None])
        single.append(1.0 / ORDER + 2.0 / ORDER * poly_there @ poly_here.T)
    rows, quarters = [], []
    for octant in range(OCTANTS):
        along = [single[octant // 4 % 2], single[octant // 2 % 2], single[octant % 2]]
        full = np.kron(np.kron(along[0], along[1]), along[2])
        rows.append(np.kron(np.eye(2), full))
        quarters.append(np.kron(np.ones((1, 2)), full))
    table = np.concatenate(rows).astype(np.float32)
    high = table.astype(bf16)
    low = (table - high.astype(np.float32)).astype(bf16)
    return np.concatenate([high, low], 1), np.concatenate(quarters).astype(np.float32)


def near_columns():
    here = points()
    index = np.arange(NODES)
    coords = np.stack([here[index // ORDER**2], here[index // ORDER % ORDER], here[index % ORDER]])
    return np.tile(NEAR * coords.reshape(-1, 1), (1, WIDTH)).astype(np.float32)


def octant_rows():
    here = points()
    index = np.arange(NODES)
    coords = np.stack([here[index // ORDER**2], here[index // ORDER % ORDER], here[index % ORDER]])
    coords = np.concatenate([coords, coords], 1)
    octant = np.arange(OCTANTS)
    signs = np.stack([octant // 4 % 2, octant // 2 % 2, octant % 2]) * 2.0 - 1.0
    near = np.tile(NEAR * signs[:, :, None], (1, 1, WIDTH))
    far = FAR * (coords[:, None, :] + signs[:, :, None])
    return np.concatenate([near, far]).astype(np.float32).reshape(-1, WIDTH)


def split(value):
    high = value.astype(bf16)
    low = (value - high.astype(f32)).astype(bf16)
    return high, low


def joined(product, rows):
    top = product[:rows]
    bottom = product[rows:]
    return top[:, :WIDTH] + (top[:, WIDTH:] + bottom[:, :WIDTH]) + bottom[:, WIDTH:]


def times(value, weights):
    high, low = split(value)
    product = jnp.dot(jnp.concatenate([high, low]), weights, preferred_element_type=f32)
    return joined(product, value.shape[0])


def leaf_kernel(
    place,
    occupied_far,
    narrow_far,
    leaves_far,
    out,
    occupied,
    narrow,
    leaves,
    weights,
    masked,
    first,
    sems,
):
    copies = [
        pltpu.make_async_copy(far, near, sems.at[i])
        for i, (far, near) in enumerate(
            ((occupied_far, occupied), (narrow_far, narrow), (leaves_far, leaves))
        )
    ]
    for copy in copies:
        copy.start()
    rows = leaves.shape[0]
    copies[0].wait()
    columns = []
    for block in range(rows // WIDTH):
        line = occupied[block : block + 1, :].astype(f32)
        columns.append(jnp.transpose(jnp.broadcast_to(line, (WIDTH, WIDTH))))
    copies[1].wait()
    real = lax.broadcasted_iota(jnp.int32, (NODES, WIDTH), 1) < NODES
    for o in range(OCTANTS):
        value = narrow[o * NODES : (o + 1) * NODES, :].astype(f32)
        other = pltpu.roll(value, NODES, 1)
        top = pl.ds(o * WIDTH, NODES)
        bottom = pl.ds(o * WIDTH + NODES, NODES)
        weights[top, :WIDTH] = jnp.where(real, value, 0.0).astype(bf16)
        weights[top, WIDTH:] = jnp.where(real, other, 0.0).astype(bf16)
        weights[bottom, :WIDTH] = jnp.where(real, 0.0, other).astype(bf16)
        weights[bottom, WIDTH:] = jnp.where(real, 0.0, value).astype(bf16)
    copies[2].wait()
    for block in range(rows // WIDTH):
        at = pl.ds(WIDTH * block, WIDTH)
        masked[at, :] = leaves[at, :] * columns[block]
    boxes = rows // OCTANTS
    parts = [masked[pl.ds(o, boxes, stride=OCTANTS), :] for o in range(OCTANTS)]
    first[...] = times(jnp.concatenate(parts, 1), weights[...])
    pairs = [first[pl.ds(r, boxes // 2, stride=2), :] for r in range(2)]
    start = pl.multiple_of(place[0] * (2 * WIDTH), 2 * WIDTH)
    own = weights[pl.ds(start, 2 * WIDTH), :]
    second = times(jnp.concatenate(pairs, 1), own)
    out[...] = second.reshape(out.shape)


def cosine_sine(x):
    turns = jnp.floor(x * (2.0 / math.pi) + 0.5)
    r = x - turns * 1.5703125
    r = r - turns * 4.837512969970703125e-4
    r = r - turns * 7.54978995489188216e-8
    z = r * r
    sine = r + r * z * (-1.6666654611e-1 + z * (8.3321608736e-3 - z * 1.9515295891e-4))
    cosine = 4.166664568298827e-2 + z * (-1.388731625493765e-3 + z * 2.443315711809948e-5)
    cosine = 1.0 - 0.5 * z + z * z * cosine
    quarter = turns.astype(jnp.int32)
    swap = (quarter & 1) == 1
    c = jnp.where(swap, sine, cosine)
    s = jnp.where(swap, cosine, sine)
    return jnp.where(((quarter + 1) & 2) == 2, -c, c), jnp.where((quarter & 2) == 2, -s, s)


def flag_columns(rows):
    count, width = rows.shape
    flags = jnp.concatenate([rows, jnp.zeros((WIDTH - count, width), f32)])
    if width < WIDTH:
        flags = jnp.concatenate([flags, jnp.zeros((WIDTH, WIDTH - width), f32)], 1)
    return jnp.transpose(flags)


def table_kernel(
    place,
    angles_far,
    three_far,
    four_far,
    fixed_far,
    high,
    low,
    far_cos,
    far_sin,
    flags,
    keep,
    angles,
    need_three,
    need_four,
    fixed,
    sems,
):
    copies = [
        pltpu.make_async_copy(far, near, sems.at[i])
        for i, (far, near) in enumerate(
            (
                (angles_far, angles),
                (three_far, need_three),
                (four_far, need_four),
                (fixed_far, fixed),
            )
        )
    ]
    for copy in copies:
        copy.start()
    cones, boxes = need_three.shape
    fours = need_four.shape[1]
    copies[1].wait()
    flags[...] = flag_columns(need_three[...].astype(f32))
    copies[2].wait()
    four_flags = flag_columns(need_four[...].astype(f32))
    for c in range(cones):
        keep[pl.ds(c * fours, fours), :] = jnp.broadcast_to(
            four_flags[:fours, c : c + 1], (fours, WIDTH)
        )
    copies[0].wait()
    row = lax.broadcasted_iota(jnp.int32, (8, WIDTH), 0)
    polar = jnp.zeros((8, WIDTH), f32)
    azimuth = jnp.zeros((8, WIDTH), f32)
    for c in range(cones):
        polar = jnp.where(row == c, angles[0, place[0] * cones + c], polar)
        azimuth = jnp.where(row == c, angles[1, place[0] * cones + c], azimuth)
    cos_p, sin_p = cosine_sine(polar)
    cos_a, sin_a = cosine_sine(azimuth)
    direction = (sin_p * cos_a, sin_p * sin_a, cos_p)
    real = lax.broadcasted_iota(jnp.int32, (NODES, WIDTH), 1) < NODES
    copies[3].wait()
    octants = 3 * NODES
    quarters = octants + 6 * OCTANTS
    for c in range(cones):
        along = [direction[d][c : c + 1, :] for d in range(3)]

        def dot(start, size):
            value = along[0] * fixed[start : start + size, :]
            value = value + along[1] * fixed[start + size : start + 2 * size, :]
            return value + along[2] * fixed[start + 2 * size : start + 3 * size, :]

        c0, s0 = cosine_sine(dot(0, NODES))
        even = jnp.where(real, c0, -s0)
        odd = jnp.where(real, -s0, -c0)
        c1, s1 = cosine_sine(dot(octants, OCTANTS))
        for o in range(OCTANTS):
            value = even * c1[o : o + 1, :] + odd * s1[o : o + 1, :]
            value = value * fixed[quarters + o * NODES : quarters + (o + 1) * NODES, :]
            top, rest = split(value)
            high[o * NODES : (o + 1) * NODES, c * WIDTH : (c + 1) * WIDTH] = top
            low[o * NODES : (o + 1) * NODES, c * WIDTH : (c + 1) * WIDTH] = rest
        c3, s3 = cosine_sine(dot(octants + 3 * OCTANTS, OCTANTS))
        far_cos[c * OCTANTS : (c + 1) * OCTANTS, :] = c3
        far_sin[c * OCTANTS : (c + 1) * OCTANTS, :] = jnp.where(real[:OCTANTS], s3, -s3)


def level_kernel(
    place, gathered, high, low, far_cos, far_sin, flags, keep, weights, out, lowfreq, turned
):
    lowfreq[...] = gathered[pl.ds(pl.multiple_of(place[0] * OCTANTS, OCTANTS), OCTANTS), :]
    boxes = gathered.shape[0] // OCTANTS
    rows = keep.shape[0]
    real = lax.broadcasted_iota(jnp.int32, (boxes, WIDTH), 1) < NODES
    reals, imags = [], []
    for o in range(0, OCTANTS, 2):
        a = gathered[pl.ds(o, boxes, stride=OCTANTS), :]
        b = gathered[pl.ds(o + 1, boxes, stride=OCTANTS), :]
        reals.append(jnp.where(real, a, pltpu.roll(b, NODES, 1)))
        imags.append(jnp.where(real, pltpu.roll(a, NODES, 1), b))
    both = jnp.concatenate([jnp.concatenate(reals, 1), jnp.concatenate(imags, 1)])
    top, rest = split(both)
    product = jnp.dot(jnp.concatenate([top, rest]), high[...], preferred_element_type=f32)
    product = product[: 2 * boxes] + (
        product[2 * boxes :] + jnp.dot(top, low[...], preferred_element_type=f32)
    )
    for c in range(product.shape[1] // WIDTH):
        part = product[:, c * WIDTH : (c + 1) * WIDTH]
        across = pltpu.roll(part[boxes:], NODES, 1)
        three = part[:boxes] + jnp.where(real, -across, across)
        three = three * jnp.broadcast_to(flags[:, c : c + 1], (boxes, WIDTH))
        at = slice(c * OCTANTS, (c + 1) * OCTANTS)
        cosine = jnp.concatenate([far_cos[at, :]] * (boxes // OCTANTS))
        sine = jnp.concatenate([far_sin[at, :]] * (boxes // OCTANTS))
        turned[pl.ds(c * boxes, boxes), :] = cosine * three + sine * pltpu.roll(three, NODES, 1)
    parts = [turned[pl.ds(o, rows, stride=OCTANTS), :] for o in range(OCTANTS)]
    four = times(jnp.concatenate(parts, 1), weights[...])
    out[...] = (four * keep[...]).reshape(out.shape)


def hbm():
    return pl.BlockSpec(memory_space=pltpu.HBM)


def vmem():
    return pl.BlockSpec(memory_space=pltpu.VMEM)


def smem():
    return pl.BlockSpec(memory_space=pltpu.SMEM)


def here(array):
    return pltpu.with_memory_space_constraint(array, pltpu.VMEM)


def local(leaf_expansions, leaf_occupied, cone_angles, cone_need3, cone_need4):
    rows, width = leaf_expansions.shape
    cones, boxes = cone_need3.shape
    fours = cone_need4.shape[1]
    subs = lax.axis_size("sub")
    blocks = lax.axis_size("z") * lax.axis_size("y")
    place = lax.axis_index(("half", "z", "y")).reshape(1)
    parts, doubled = transfer_rows()
    weights = jnp.asarray(parts)
    narrow = parts.reshape(OCTANTS, 2, NODES, 4, NODES)[:, 0, :, ::2].reshape(-1, width)
    partial = pl.pallas_call(
        leaf_kernel,
        out_shape=jax.ShapeDtypeStruct((subs, 8, width), f32),
        in_specs=[smem(), hbm(), hbm(), hbm()],
        out_specs=vmem(),
        scratch_shapes=[
            pltpu.VMEM((rows // width, width), jnp.int32),
            pltpu.VMEM(narrow.shape, bf16),
            pltpu.VMEM((rows, width), f32),
            pltpu.VMEM(parts.shape, bf16),
            pltpu.VMEM((rows, width), f32),
            pltpu.VMEM((rows // 8, width), f32),
            pltpu.SemaphoreType.DMA((3,)),
        ],
        compiler_params=pltpu.CompilerParams(vmem_limit_bytes=60 << 20),
        name="leaves",
    )(
        lax.axis_index("sub").reshape(1),
        leaf_occupied.reshape(rows // 128, 128),
        jnp.asarray(narrow),
        leaf_expansions,
    )
    received = lax.all_to_all(partial, "sub", split_axis=0, concat_axis=0, tiled=True)
    fixed = np.concatenate([near_columns(), octant_rows(), doubled])
    tables = pl.pallas_call(
        table_kernel,
        out_shape=[
            pltpu.VMEM((OCTANTS * NODES, cones * width), bf16),
            pltpu.VMEM((OCTANTS * NODES, cones * width), bf16),
            pltpu.VMEM((cones * OCTANTS, width), f32),
            pltpu.VMEM((cones * OCTANTS, width), f32),
            pltpu.VMEM((boxes, width), f32),
            pltpu.VMEM((cones * fours, width), f32),
        ],
        in_specs=[smem()] + [hbm()] * 4,
        out_specs=[vmem()] * 6,
        scratch_shapes=[
            pltpu.SMEM(cone_angles.shape, f32),
            pltpu.VMEM(cone_need3.shape, jnp.int32),
            pltpu.VMEM(cone_need4.shape, jnp.int32),
            pltpu.VMEM(fixed.shape, f32),
            pltpu.SemaphoreType.DMA((4,)),
        ],
        compiler_params=pltpu.CompilerParams(vmem_limit_bytes=60 << 20),
        name="tables",
    )(
        place,
        cone_angles,
        cone_need3,
        cone_need4,
        jnp.asarray(fixed),
    )
    received, *tables = lax.optimization_barrier((received, *tables))
    gathered = lax.all_to_all(
        jnp.broadcast_to(received.sum(axis=0)[None], (blocks, 8, width)),
        ("z", "y"),
        split_axis=0,
        concat_axis=0,
        tiled=True,
    )
    gathered = lax.all_gather(gathered.reshape(blocks * 8, width), "half", tiled=True)
    cone_expansions, lowfreq = pl.pallas_call(
        level_kernel,
        out_shape=[
            jax.ShapeDtypeStruct((cones, fours, width), f32),
            jax.ShapeDtypeStruct((8, width), f32),
        ],
        in_specs=[smem()] + [vmem()] * 8,
        out_specs=[vmem(), vmem()],
        scratch_shapes=[pltpu.VMEM((cones * boxes, width), f32)],
        compiler_params=pltpu.CompilerParams(vmem_limit_bytes=24 << 20),
        name="levels",
    )(place, here(gathered), *[here(table) for table in tables], weights)
    return (lowfreq, cone_expansions)


def solution(mesh):
    halves, blocks, subs = mesh.devices.shape
    fine = Mesh(
        mesh.devices.reshape(halves, blocks // OCTANTS, OCTANTS, subs), ("half", "z", "y", "sub")
    )
    blk = ("half", "z", "y")
    return jax.shard_map(
        local,
        mesh=fine,
        in_specs=(
            P(blk + ("sub",), None),
            P(blk + ("sub",)),
            P(),
            P(blk, "sub"),
            P(blk, "sub"),
        ),
        out_specs=(P(blk + ("sub",), None), P(blk, "sub", None)),
        check_vma=False,
    )
```

time: 53.8 us -> 48.2 us (0.90)
  local copies, waits for them, and re-layouts: 8.59 us -> 0.03 us
  waiting for transfers between devices: 0.01 us -> 2.28 us
  Pallas kernels: 5.14 us -> 6.09 us
    unnamed x26 -> x2, local copies, waits for them, and re-layouts: 8.57 us -> 0.01 us
    all_to_all x1, waiting for transfers between devices: 0.01 us -> 2.28 us  [local(): lax.all_to_all(partial, 'sub', split_axis=0, concat_axis=0, tiled=True)]
    pallas_call x1, Pallas kernels: 1.09 us -> 2.07 us  [local(): pl.pallas_call(leaf_kernel, out_shape=jax.ShapeDtypeStruct((subs, 8, widt...]
  transfers between devices with their start and end apart: 1 -> 1, of which waited for: 0 -> 1; matrix products, arithmetic and copies ran while one was open for 0% -> 0% of each run, Pallas kernels for 4% -> 4%
where the time goes in v3:
time: 48.2 us; the launch traced here: 48 us
  blocking collectives  34.1 us (71%)
  Pallas kernels  6.09 us (13%)
  starting transfers between devices  4.85 us (10%)
  waiting for transfers between devices  2.28 us (5%)
  between operations  0.66 us (1%)
    all_to_all x1, blocking collectives, local(): lax.all_to_all(jnp.broadcast_to(received.sum(axis=0)[None], (blocks, 8, w...  28.6 us
    all_gather x1, blocking collectives, local(): lax.all_gather(gathered.reshape(blocks * 8, width), 'half', tiled=True)  5.48 us
    all_to_all x1, starting transfers between devices, local(): lax.all_to_all(partial, 'sub', split_axis=0, concat_axis=0, tiled=True)  4.85 us
    all_to_all x1, waiting for transfers between devices, local(): lax.all_to_all(partial, 'sub', split_axis=0, concat_axis=0, tiled=True)  2.28 us
    pallas_call x1, Pallas kernels, local(): pl.pallas_call(level_kernel, out_shape=[jax.ShapeDtypeStruct((cones, four...  2.09 us
    pallas_call x1, Pallas kernels, local(): pl.pallas_call(leaf_kernel, out_shape=jax.ShapeDtypeStruct((subs, 8, widt...  2.07 us
    pallas_call x1, Pallas kernels, local(): pl.pallas_call(table_kernel, out_shape=[pltpu.VMEM((OCTANTS * NODES, cone...  1.92 us
  transfers between devices with their start and end apart: 1, of which 1 were waited for; matrix products, arithmetic and copies ran while one was open for 0% of the time, Pallas kernels for 4%

profile of v3, /device:TPU:1, one launch (start us, length us, event | category | flops | bytes accessed | tf_op | source)
XLA Modules:
  0.0 48.0 jit_solution(8602285816008216075)
XLA Ops:
  0.6 2.1 %leaves.1 = f32[4,8,128]{2,1,0:T(8,128)} custom-call(s32[1]{0:T(128)} %bitcast.1.place, s32[4,128]{1,0:T(4,128)} %bitcast.5, bf16[512,128]{1,0:T(8,128)(2,1)} %constant.32.clone.narrow_far, f32[512,128]{1,0:T(8,128)} %leaves_far.1), custom_call_target="tpu_custom_call" | custom-call | tf_op jit(solution)/shard_map/leaves/pallas_call | solution.py:299
  2.7 4.9 %all-to-all-start = ((f32[4,8,128]{2,1,0:T(8,128)}), f32[4,8,128]{2,1,0:T(8,128)S(1)}, u32[]{:S(2)}, u32[]{:S(2)}) async-start(f32[4,8,128]{2,1,0:T(8,128)} %leaves.1), calls=%async_computation | async-start | bytes 32768 | tf_op jit(solution)/shard_map/all_to_all | solution.py:321
  7.6 1.9 %tables.1 = (bf16[512,768]{1,0:T(8,128)(2,1)S(1)}, bf16[512,768]{1,0:T(8,128)(2,1)S(1)}, f32[48,128]{1,0:T(8,128)S(1)}, f32[48,128]{1,0:T(8,128)S(1)}, f32[128,128]{1,0:T(8,128)S(1)}, /*index=5*/f32[96,128]{1,0:T(8,128)S(1)}) custom-call(s32[1]{0:T(128)} %bitcast.place, f32[2,768]{1,0:T(2,128)} %angles_far.1, s32[6,128]{1,0:T(8,128)} %three_far.1, ...), custom_call_target="tpu_custom_call" | custom-call | tf_op jit(solution)/shard_map/tables/pallas_call | solution.py:323
  9.5 2.3 %all-to-all-done = f32[4,8,128]{2,1,0:T(8,128)S(1)} async-done(((f32[4,8,128]{2,1,0:T(8,128)}), f32[4,8,128]{2,1,0:T(8,128)S(1)}, u32[]{:S(2)}, u32[]{:S(2)}) %all-to-all-start) | async-done | bytes 16416 | tf_op jit(solution)/shard_map/all_to_all | solution.py:321
  11.8 28.6 %all_to_all.10 = f32[64,8,128]{2,1,0:T(8,128)S(1)} all-to-all(f32[64,8,128]{2,1,0:T(8,128)S(1)} %broadcast_in_dim.2), channel_id=1, replica_groups=mesh['half'=2,'z'=8,'y'=8,'sub'=4] {'z','y'}, dimensions={0} | all-to-all | bytes 524288 | tf_op jit(solution)/shard_map/all_to_all | solution.py:352
  40.4 0.0 copy-start
  40.4 5.5 %all_gather.3.gathered = f32[1024,128]{1,0:T(8,128)S(1)} all-gather(f32[512,128]{1,0:T(8,128)S(1)} %bitcast.4), channel_id=1, replica_groups=mesh['half'=2,'z'=8,'y'=8,'sub'=4] {'half'}, dimensions={0}, use_global_device_ids=true | all-gather | bytes 786432 | tf_op jit(solution)/shard_map/all_gather | solution.py:359
  45.9 0.0 copy-done
  45.9 2.1 %levels.1 = (f32[6,16,128]{2,1,0:T(8,128)}, f32[8,128]{1,0:T(8,128)}) custom-call(s32[1]{0:T(128)} %bitcast.place, f32[1024,128]{1,0:T(8,128)S(1)} %all_gather.3.gathered, bf16[512,768]{1,0:T(8,128)(2,1)S(1)} %get-tuple-element.24.high, bf16[512,768]{1,0:T(8,128)(2,1)S(1)} %get-tuple-element.25.low, f32[48,128]{1,0:T(8,128)S(1)} %get-tuple-element.26.far_cos, ...), custom_call_target="tpu_custom_call" | custom-call | tf_op jit(solution)/shard_map/levels/pallas_call | solution.py:360
  (2 shorter events, 0.0 us)
Async XLA Ops:
  2.7 9.1 %all-to-all-start = ((f32[4,8,128]{2,1,0:T(8,128)}), f32[4,8,128]{2,1,0:T(8,128)S(1)}, u32[]{:S(2)}, u32[]{:S(2)}) async-start(f32[4,8,128]{2,1,0:T(8,128)} %leaves.1), calls=%async_computation | async-start | bytes 32768 | tf_op jit(solution)/shard_map/all_to_all | solution.py:321
  40.4 5.5 %copy-start = (bf16[1024,256]{1,0:T(8,128)(2,1)S(1)}, bf16[1024,256]{1,0:T(8,128)(2,1)}, u32[]{:S(2)}) copy-start(bf16[1024,256]{1,0:T(8,128)(2,1)} %constant.31.clone.weights) | copy-start | bytes 1572868

commit v4 on v3

--- a/solution.py
+++ b/solution.py
@@ -80,6 +80,13 @@
     high, low = split(value)
     product = jnp.dot(jnp.concatenate([high, low]), weights, preferred_element_type=f32)
     return joined(product, value.shape[0])
+
+
+def packed(even, odd):
+    real = lax.broadcasted_iota(jnp.int32, even.shape, 1) < NODES
+    reals = jnp.where(real, even, pltpu.roll(odd, NODES, 1))
+    imags = jnp.where(real, pltpu.roll(even, NODES, 1), odd)
+    return reals, imags
 
 
 def leaf_kernel(
@@ -132,7 +139,13 @@
     start = pl.multiple_of(place[0] * (2 * WIDTH), 2 * WIDTH)
     own = weights[pl.ds(start, 2 * WIDTH), :]
     second = times(jnp.concatenate(pairs, 1), own)
-    out[...] = second.reshape(out.shape)
+    count = second.shape[0]
+    first[pl.ds(0, count), :] = second
+    reals, imags = packed(*[first[pl.ds(i, count // 2, stride=2), :] for i in range(2)])
+    for s in range(out.shape[0]):
+        at = slice(s * OCTANTS // 2, (s + 1) * OCTANTS // 2)
+        out[s, : OCTANTS // 2, :] = reals[at]
+        out[s, OCTANTS // 2 :, :] = imags[at]
 
 
 def cosine_sine(x):
@@ -169,7 +182,6 @@
     low,
     far_cos,
     far_sin,
-    flags,
     keep,
     angles,
     need_three,
@@ -193,7 +205,7 @@
     cones, boxes = need_three.shape
     fours = need_four.shape[1]
     copies[1].wait()
-    flags[...] = flag_columns(need_three[...].astype(f32))
+    three_flags = flag_columns(need_three[...].astype(f32))
     copies[2].wait()
     four_flags = flag_columns(need_four[...].astype(f32))
     for c in range(cones):
@@ -233,38 +245,46 @@
             high[o * NODES : (o + 1) * NODES, c * WIDTH : (c + 1) * WIDTH] = top
             low[o * NODES : (o + 1) * NODES, c * WIDTH : (c + 1) * WIDTH] = rest
         c3, s3 = cosine_sine(dot(octants + 3 * OCTANTS, OCTANTS))
-        far_cos[c * OCTANTS : (c + 1) * OCTANTS, :] = c3
-        far_sin[c * OCTANTS : (c + 1) * OCTANTS, :] = jnp.where(real[:OCTANTS], s3, -s3)
+        column = jnp.broadcast_to(three_flags[:, c : c + 1], (boxes, WIDTH))
+        at = pl.ds(c * boxes, boxes)
+        far_cos[at, :] = jnp.concatenate([c3] * (boxes // OCTANTS)) * column
+        far_sin[at, :] = jnp.concatenate([s3] * (boxes // OCTANTS)) * column
 
 
 def level_kernel(
-    place, gathered, high, low, far_cos, far_sin, flags, keep, weights, out, lowfreq, turned
+    place, gathered, high, low, far_cos, far_sin, keep, weights, out, lowfreq, turned
 ):
-    lowfreq[...] = gathered[pl.ds(pl.multiple_of(place[0] * OCTANTS, OCTANTS), OCTANTS), :]
     boxes = gathered.shape[0] // OCTANTS
     rows = keep.shape[0]
-    real = lax.broadcasted_iota(jnp.int32, (boxes, WIDTH), 1) < NODES
-    reals, imags = [], []
-    for o in range(0, OCTANTS, 2):
-        a = gathered[pl.ds(o, boxes, stride=OCTANTS), :]
-        b = gathered[pl.ds(o + 1, boxes, stride=OCTANTS), :]
-        reals.append(jnp.where(real, a, pltpu.roll(b, NODES, 1)))
-        imags.append(jnp.where(real, pltpu.roll(a, NODES, 1), b))
-    both = jnp.concatenate([jnp.concatenate(reals, 1), jnp.concatenate(imags, 1)])
+    half = OCTANTS // 2
+    own = gathered[pl.ds(pl.multiple_of(place[0] * OCTANTS, OCTANTS), OCTANTS), :]
+    even, odd = packed(own[:half], own[half:])
+    for p in range(half):
+        lowfreq[2 * p : 2 * p + 1, :] = even[p : p + 1]
+        lowfreq[2 * p + 1 : 2 * p + 2, :] = odd[p : p + 1]
+    both = jnp.concatenate(
+        [
+            jnp.concatenate(
+                [gathered[pl.ds(i * half + p, boxes, stride=OCTANTS), :] for p in range(half)], 1
+            )
+            for i in range(2)
+        ]
+    )
     top, rest = split(both)
     product = jnp.dot(jnp.concatenate([top, rest]), high[...], preferred_element_type=f32)
     product = product[: 2 * boxes] + (
         product[2 * boxes :] + jnp.dot(top, low[...], preferred_element_type=f32)
     )
+    real = lax.broadcasted_iota(jnp.int32, (boxes, WIDTH), 1) < NODES
+    sign = jnp.where(real, 1.0, -1.0)
     for c in range(product.shape[1] // WIDTH):
-        part = product[:, c * WIDTH : (c + 1) * WIDTH]
-        across = pltpu.roll(part[boxes:], NODES, 1)
-        three = part[:boxes] + jnp.where(real, -across, across)
-        three = three * jnp.broadcast_to(flags[:, c : c + 1], (boxes, WIDTH))
-        at = slice(c * OCTANTS, (c + 1) * OCTANTS)
-        cosine = jnp.concatenate([far_cos[at, :]] * (boxes // OCTANTS))
-        sine = jnp.concatenate([far_sin[at, :]] * (boxes // OCTANTS))
-        turned[pl.ds(c * boxes, boxes), :] = cosine * three + sine * pltpu.roll(three, NODES, 1)
+        reals = product[:boxes, c * WIDTH : (c + 1) * WIDTH]
+        imags = product[boxes:, c * WIDTH : (c + 1) * WIDTH]
+        at = pl.ds(c * boxes, boxes)
+        cosine = far_cos[at, :]
+        sine = far_sin[at, :]
+        across = (cosine * imags - sine * reals) * sign
+        turned[at, :] = (cosine * reals + sine * imags) + pltpu.roll(across, NODES, 1)
     parts = [turned[pl.ds(o, rows, stride=OCTANTS), :] for o in range(OCTANTS)]
     four = times(jnp.concatenate(parts, 1), weights[...])
     out[...] = (four * keep[...]).reshape(out.shape)
@@ -325,13 +345,12 @@
         out_shape=[
             pltpu.VMEM((OCTANTS * NODES, cones * width), bf16),
             pltpu.VMEM((OCTANTS * NODES, cones * width), bf16),
-            pltpu.VMEM((cones * OCTANTS, width), f32),
-            pltpu.VMEM((cones * OCTANTS, width), f32),
-            pltpu.VMEM((boxes, width), f32),
+            pltpu.VMEM((cones * boxes, width), f32),
+            pltpu.VMEM((cones * boxes, width), f32),
             pltpu.VMEM((cones * fours, width), f32),
         ],
         in_specs=[smem()] + [hbm()] * 4,
-        out_specs=[vmem()] * 6,
+        out_specs=[vmem()] * 5,
         scratch_shapes=[
             pltpu.SMEM(cone_angles.shape, f32),
             pltpu.VMEM(cone_need3.shape, jnp.int32),
@@ -363,7 +382,7 @@
             jax.ShapeDtypeStruct((cones, fours, width), f32),
             jax.ShapeDtypeStruct((8, width), f32),
         ],
-        in_specs=[smem()] + [vmem()] * 8,
+        in_specs=[smem()] + [vmem()] * 7,
         out_specs=[vmem(), vmem()],
         scratch_shapes=[pltpu.VMEM((cones * boxes, width), f32)],
         compiler_params=pltpu.CompilerParams(vmem_limit_bytes=24 << 20),

time: 48.2 us -> 48.1 us (level)
  no operation moved by 1% of the time
where the time goes in v4:
time: 48.1 us; the launch traced here: 47.9 us
  blocking collectives  34.1 us (71%)
  Pallas kernels  6.03 us (13%)
  starting transfers between devices  4.85 us (10%)
  waiting for transfers between devices  2.22 us (5%)
  between operations  0.66 us (1%)
    all_to_all x1, blocking collectives, local(): lax.all_to_all(jnp.broadcast_to(received.sum(axis=0)[None], (blocks, 8, w...  28.6 us
    all_gather x1, blocking collectives, local(): lax.all_gather(gathered.reshape(blocks * 8, width), 'half', tiled=True)  5.48 us
    all_to_all x1, starting transfers between devices, local(): lax.all_to_all(partial, 'sub', split_axis=0, concat_axis=0, tiled=True)  4.85 us
    all_to_all x1, waiting for transfers between devices, local(): lax.all_to_all(partial, 'sub', split_axis=0, concat_axis=0, tiled=True)  2.22 us
    pallas_call x1, Pallas kernels, local(): pl.pallas_call(leaf_kernel, out_shape=jax.ShapeDtypeStruct((subs, 8, widt...  2.15 us
    pallas_call x1, Pallas kernels, local(): pl.pallas_call(table_kernel, out_shape=[pltpu.VMEM((OCTANTS * NODES, cone...  1.98 us
    pallas_call x1, Pallas kernels, local(): pl.pallas_call(level_kernel, out_shape=[jax.ShapeDtypeStruct((cones, four...  1.91 us
  transfers between devices with their start and end apart: 1, of which 1 were waited for; matrix products, arithmetic and copies ran while one was open for 0% of the time, Pallas kernels for 4%

profile of v4, /device:TPU:1, one launch (start us, length us, event | category | flops | bytes accessed | tf_op | source)
XLA Modules:
  0.0 47.9 jit_solution(8484368095254203169)
XLA Ops:
  0.6 2.1 %leaves.1 = f32[4,8,128]{2,1,0:T(8,128)} custom-call(s32[1]{0:T(128)} %bitcast.1.place, s32[4,128]{1,0:T(4,128)} %bitcast.5, bf16[512,128]{1,0:T(8,128)(2,1)} %constant.32.clone.narrow_far, f32[512,128]{1,0:T(8,128)} %leaves_far.1), custom_call_target="tpu_custom_call" | custom-call | tf_op jit(solution)/shard_map/leaves/pallas_call | solution.py:319
  2.8 4.9 %all-to-all-start = ((f32[4,8,128]{2,1,0:T(8,128)}), f32[4,8,128]{2,1,0:T(8,128)S(1)}, u32[]{:S(2)}, u32[]{:S(2)}) async-start(f32[4,8,128]{2,1,0:T(8,128)} %leaves.1), calls=%async_computation | async-start | bytes 32768 | tf_op jit(solution)/shard_map/all_to_all | solution.py:341
  7.6 2.0 %tables.1 = (bf16[512,768]{1,0:T(8,128)(2,1)S(1)}, bf16[512,768]{1,0:T(8,128)(2,1)S(1)}, f32[768,128]{1,0:T(8,128)S(1)}, f32[768,128]{1,0:T(8,128)S(1)}, f32[96,128]{1,0:T(8,128)S(1)}) custom-call(s32[1]{0:T(128)} %bitcast.place, f32[2,768]{1,0:T(2,128)} %angles_far.1, s32[6,128]{1,0:T(8,128)} %three_far.1, s32[6,16]{1,0:T(8,128)} %four_far.1, ...), custom_call_target="tpu_custom_call" | custom-call | tf_op jit(solution)/shard_map/tables/pallas_call | solution.py:343
  9.6 2.2 %all-to-all-done = f32[4,8,128]{2,1,0:T(8,128)S(1)} async-done(((f32[4,8,128]{2,1,0:T(8,128)}), f32[4,8,128]{2,1,0:T(8,128)S(1)}, u32[]{:S(2)}, u32[]{:S(2)}) %all-to-all-start) | async-done | bytes 16416 | tf_op jit(solution)/shard_map/all_to_all | solution.py:341
  11.9 28.6 %all_to_all.10 = f32[64,8,128]{2,1,0:T(8,128)S(1)} all-to-all(f32[64,8,128]{2,1,0:T(8,128)S(1)} %broadcast_in_dim.2), channel_id=1, replica_groups=mesh['half'=2,'z'=8,'y'=8,'sub'=4] {'z','y'}, dimensions={0} | all-to-all | bytes 524288 | tf_op jit(solution)/shard_map/all_to_all | solution.py:371
  40.5 0.0 copy-start
  40.5 5.5 %all_gather.3.gathered = f32[1024,128]{1,0:T(8,128)S(1)} all-gather(f32[512,128]{1,0:T(8,128)S(1)} %bitcast.4), channel_id=1, replica_groups=mesh['half'=2,'z'=8,'y'=8,'sub'=4] {'half'}, dimensions={0}, use_global_device_ids=true | all-gather | bytes 786432 | tf_op jit(solution)/shard_map/all_gather | solution.py:378
  46.0 0.0 copy-done
  46.0 1.9 %levels.1 = (f32[6,16,128]{2,1,0:T(8,128)}, f32[8,128]{1,0:T(8,128)}) custom-call(s32[1]{0:T(128)} %bitcast.place, f32[1024,128]{1,0:T(8,128)S(1)} %all_gather.3.gathered, bf16[512,768]{1,0:T(8,128)(2,1)S(1)} %get-tuple-element.21.high, bf16[512,768]{1,0:T(8,128)(2,1)S(1)} %get-tuple-element.22.low, f32[768,128]{1,0:T(8,128)S(1)} %get-tuple-element.23.far_cos, ...), custom_call_target="tpu_custom_call" | custom-call | tf_op jit(solution)/shard_map/levels/pallas_call | solution.py:379
  (2 shorter events, 0.0 us)
Async XLA Ops:
  2.8 9.1 %all-to-all-start = ((f32[4,8,128]{2,1,0:T(8,128)}), f32[4,8,128]{2,1,0:T(8,128)S(1)}, u32[]{:S(2)}, u32[]{:S(2)}) async-start(f32[4,8,128]{2,1,0:T(8,128)} %leaves.1), calls=%async_computation | async-start | bytes 32768 | tf_op jit(solution)/shard_map/all_to_all | solution.py:341
  40.5 5.5 %copy-start = (bf16[1024,256]{1,0:T(8,128)(2,1)S(1)}, bf16[1024,256]{1,0:T(8,128)(2,1)}, u32[]{:S(2)}) copy-start(bf16[1024,256]{1,0:T(8,128)(2,1)} %constant.31.clone.weights) | copy-start | bytes 1572868

commit v5 on v4

--- a/solution.py
+++ b/solution.py
@@ -90,7 +90,6 @@
 
 
 def leaf_kernel(
-    place,
     occupied_far,
     narrow_far,
     leaves_far,
@@ -136,7 +135,7 @@
     parts = [masked[pl.ds(o, boxes, stride=OCTANTS), :] for o in range(OCTANTS)]
     first[...] = times(jnp.concatenate(parts, 1), weights[...])
     pairs = [first[pl.ds(r, boxes // 2, stride=2), :] for r in range(2)]
-    start = pl.multiple_of(place[0] * (2 * WIDTH), 2 * WIDTH)
+    start = pl.multiple_of(lax.axis_index("sub") * (2 * WIDTH), 2 * WIDTH)
     own = weights[pl.ds(start, 2 * WIDTH), :]
     second = times(jnp.concatenate(pairs, 1), own)
     count = second.shape[0]
@@ -173,7 +172,6 @@
 
 
 def table_kernel(
-    place,
     angles_far,
     three_far,
     four_far,
@@ -214,11 +212,12 @@
         )
     copies[0].wait()
     row = lax.broadcasted_iota(jnp.int32, (8, WIDTH), 0)
+    start = lax.axis_index(("half", "z", "y")) * cones
     polar = jnp.zeros((8, WIDTH), f32)
     azimuth = jnp.zeros((8, WIDTH), f32)
     for c in range(cones):
-        polar = jnp.where(row == c, angles[0, place[0] * cones + c], polar)
-        azimuth = jnp.where(row == c, angles[1, place[0] * cones + c], azimuth)
+        polar = jnp.where(row == c, angles[0, start + c], polar)
+        azimuth = jnp.where(row == c, angles[1, start + c], azimuth)
     cos_p, sin_p = cosine_sine(polar)
     cos_a, sin_a = cosine_sine(azimuth)
     direction = (sin_p * cos_a, sin_p * sin_a, cos_p)
@@ -252,12 +251,13 @@
 
 
 def level_kernel(
-    place, gathered, high, low, far_cos, far_sin, keep, weights, out, lowfreq, turned
+    gathered, high, low, far_cos, far_sin, keep, weights, out, lowfreq, turned
 ):
     boxes = gathered.shape[0] // OCTANTS
     rows = keep.shape[0]
     half = OCTANTS // 2
-    own = gathered[pl.ds(pl.multiple_of(place[0] * OCTANTS, OCTANTS), OCTANTS), :]
+    start = pl.multiple_of(lax.axis_index(("half", "z", "y")) * OCTANTS, OCTANTS)
+    own = gathered[pl.ds(start, OCTANTS), :]
     even, odd = packed(own[:half], own[half:])
     for p in range(half):
         lowfreq[2 * p : 2 * p + 1, :] = even[p : p + 1]
@@ -298,10 +298,6 @@
     return pl.BlockSpec(memory_space=pltpu.VMEM)
 
 
-def smem():
-    return pl.BlockSpec(memory_space=pltpu.SMEM)
-
-
 def here(array):
     return pltpu.with_memory_space_constraint(array, pltpu.VMEM)
 
@@ -312,14 +308,13 @@
     fours = cone_need4.shape[1]
     subs = lax.axis_size("sub")
     blocks = lax.axis_size("z") * lax.axis_size("y")
-    place = lax.axis_index(("half", "z", "y")).reshape(1)
     parts, doubled = transfer_rows()
     weights = jnp.asarray(parts)
     narrow = parts.reshape(OCTANTS, 2, NODES, 4, NODES)[:, 0, :, ::2].reshape(-1, width)
     partial = pl.pallas_call(
         leaf_kernel,
         out_shape=jax.ShapeDtypeStruct((subs, 8, width), f32),
-        in_specs=[smem(), hbm(), hbm(), hbm()],
+        in_specs=[hbm()] * 3,
         out_specs=vmem(),
         scratch_shapes=[
             pltpu.VMEM((rows // width, width), jnp.int32),
@@ -333,7 +328,6 @@
         compiler_params=pltpu.CompilerParams(vmem_limit_bytes=60 << 20),
         name="leaves",
     )(
-        lax.axis_index("sub").reshape(1),
         leaf_occupied.reshape(rows // 128, 128),
         jnp.asarray(narrow),
         leaf_expansions,
@@ -349,7 +343,7 @@
             pltpu.VMEM((cones * boxes, width), f32),
             pltpu.VMEM((cones * fours, width), f32),
         ],
-        in_specs=[smem()] + [hbm()] * 4,
+        in_specs=[hbm()] * 4,
         out_specs=[vmem()] * 5,
         scratch_shapes=[
             pltpu.SMEM(cone_angles.shape, f32),
@@ -361,7 +355,6 @@
         compiler_params=pltpu.CompilerParams(vmem_limit_bytes=60 << 20),
         name="tables",
     )(
-        place,
         cone_angles,
         cone_need3,
         cone_need4,
@@ -382,12 +375,12 @@
             jax.ShapeDtypeStruct((cones, fours, width), f32),
             jax.ShapeDtypeStruct((8, width), f32),
         ],
-        in_specs=[smem()] + [vmem()] * 7,
+        in_specs=[vmem()] * 7,
         out_specs=[vmem(), vmem()],
         scratch_shapes=[pltpu.VMEM((cones * boxes, width), f32)],
         compiler_params=pltpu.CompilerParams(vmem_limit_bytes=24 << 20),
         name="levels",
-    )(place, here(gathered), *[here(table) for table in tables], weights)
+    )(here(gathered), *[here(table) for table in tables], weights)
     return (lowfreq, cone_expansions)
 
 

time: 48.1 us -> 48.1 us (level)
  no operation moved by 1% of the time
where the time goes in v5:
time: 48.1 us; the launch traced here: 47.9 us
  blocking collectives  34.1 us (71%)
  Pallas kernels  6.03 us (13%)
  starting transfers between devices  4.85 us (10%)
  waiting for transfers between devices  2.22 us (5%)
  between operations  0.65 us (1%)
    all_to_all x1, blocking collectives, local(): lax.all_to_all(jnp.broadcast_to(received.sum(axis=0)[None], (blocks, 8, w...  28.6 us
    all_gather x1, blocking collectives, local(): lax.all_gather(gathered.reshape(blocks * 8, width), 'half', tiled=True)  5.48 us
    all_to_all x1, starting transfers between devices, local(): lax.all_to_all(partial, 'sub', split_axis=0, concat_axis=0, tiled=True)  4.85 us
    all_to_all x1, waiting for transfers between devices, local(): lax.all_to_all(partial, 'sub', split_axis=0, concat_axis=0, tiled=True)  2.22 us
    pallas_call x1, Pallas kernels, local(): pl.pallas_call(leaf_kernel, out_shape=jax.ShapeDtypeStruct((subs, 8, widt...  2.15 us
    pallas_call x1, Pallas kernels, local(): pl.pallas_call(table_kernel, out_shape=[pltpu.VMEM((OCTANTS * NODES, cone...  1.98 us
    pallas_call x1, Pallas kernels, local(): pl.pallas_call(level_kernel, out_shape=[jax.ShapeDtypeStruct((cones, four...  1.91 us
  transfers between devices with their start and end apart: 1, of which 1 were waited for; matrix products, arithmetic and copies ran while one was open for 0% of the time, Pallas kernels for 4%

profile of v5, /device:TPU:1, one launch (start us, length us, event | category | flops | bytes accessed | tf_op | source)
XLA Modules:
  0.0 47.9 jit_solution(10277824753157422044)
XLA Ops:
  0.6 2.1 %leaves.1 = f32[4,8,128]{2,1,0:T(8,128)} custom-call(s32[4,128]{1,0:T(4,128)} %bitcast.3, bf16[512,128]{1,0:T(8,128)(2,1)} %constant.9.clone.narrow_far, f32[512,128]{1,0:T(8,128)} %leaves_far.1), custom_call_target="tpu_custom_call" | custom-call | tf_op jit(solution)/shard_map/leaves/pallas_call | solution.py:314
  2.8 4.9 %all-to-all-start = ((f32[4,8,128]{2,1,0:T(8,128)}), f32[4,8,128]{2,1,0:T(8,128)S(1)}, u32[]{:S(2)}, u32[]{:S(2)}) async-start(f32[4,8,128]{2,1,0:T(8,128)} %leaves.1), calls=%async_computation | async-start | bytes 32768 | tf_op jit(solution)/shard_map/all_to_all | solution.py:335
  7.6 2.0 %tables.1 = (bf16[512,768]{1,0:T(8,128)(2,1)S(1)}, bf16[512,768]{1,0:T(8,128)(2,1)S(1)}, f32[768,128]{1,0:T(8,128)S(1)}, f32[768,128]{1,0:T(8,128)S(1)}, f32[96,128]{1,0:T(8,128)S(1)}) custom-call(f32[2,768]{1,0:T(2,128)} %angles_far.1, s32[6,128]{1,0:T(8,128)} %three_far.1, s32[6,16]{1,0:T(8,128)} %four_far.1, f32[752,128]{1,0:T(8,128)} %constant.10.clone.fixed_far), custom_call_target="tpu_custom_call" | custom-call | tf_op jit(solution)/shard_map/tables/pallas_call | solution.py:337
  9.6 2.2 %all-to-all-done = f32[4,8,128]{2,1,0:T(8,128)S(1)} async-done(((f32[4,8,128]{2,1,0:T(8,128)}), f32[4,8,128]{2,1,0:T(8,128)S(1)}, u32[]{:S(2)}, u32[]{:S(2)}) %all-to-all-start) | async-done | bytes 16416 | tf_op jit(solution)/shard_map/all_to_all | solution.py:335
  11.9 28.6 %all_to_all.10 = f32[64,8,128]{2,1,0:T(8,128)S(1)} all-to-all(f32[64,8,128]{2,1,0:T(8,128)S(1)} %broadcast_in_dim.2), channel_id=1, replica_groups=mesh['half'=2,'z'=8,'y'=8,'sub'=4] {'z','y'}, dimensions={0} | all-to-all | bytes 524288 | tf_op jit(solution)/shard_map/all_to_all | solution.py:364
  40.5 0.0 copy-start
  40.5 5.5 %all_gather.3.gathered = f32[1024,128]{1,0:T(8,128)S(1)} all-gather(f32[512,128]{1,0:T(8,128)S(1)} %bitcast.2), channel_id=1, replica_groups=mesh['half'=2,'z'=8,'y'=8,'sub'=4] {'half'}, dimensions={0}, use_global_device_ids=true | all-gather | bytes 786432 | tf_op jit(solution)/shard_map/all_gather | solution.py:371
  46.0 0.0 copy-done
  46.0 1.9 %levels.1 = (f32[6,16,128]{2,1,0:T(8,128)}, f32[8,128]{1,0:T(8,128)}) custom-call(f32[1024,128]{1,0:T(8,128)S(1)} %all_gather.3.gathered, bf16[512,768]{1,0:T(8,128)(2,1)S(1)} %get-tuple-element.21.high, bf16[512,768]{1,0:T(8,128)(2,1)S(1)} %get-tuple-element.22.low, f32[768,128]{1,0:T(8,128)S(1)} %get-tuple-element.23.far_cos, ...), custom_call_target="tpu_custom_call" | custom-call | tf_op jit(solution)/shard_map/levels/pallas_call | solution.py:372
  (2 shorter events, 0.0 us)
Async XLA Ops:
  2.8 9.1 %all-to-all-start = ((f32[4,8,128]{2,1,0:T(8,128)}), f32[4,8,128]{2,1,0:T(8,128)S(1)}, u32[]{:S(2)}, u32[]{:S(2)}) async-start(f32[4,8,128]{2,1,0:T(8,128)} %leaves.1), calls=%async_computation | async-start | bytes 32768 | tf_op jit(solution)/shard_map/all_to_all | solution.py:335
  40.5 5.5 %copy-start = (bf16[1024,256]{1,0:T(8,128)(2,1)S(1)}, bf16[1024,256]{1,0:T(8,128)(2,1)}, u32[]{:S(2)}) copy-start(bf16[1024,256]{1,0:T(8,128)(2,1)} %constant.8.clone.weights) | copy-start | bytes 1572868

commit v6 on v5

--- a/solution.py
+++ b/solution.py
@@ -171,6 +171,13 @@
     return jnp.transpose(flags)
 
 
+def by_octant(rows, boxes):
+    share = boxes // OCTANTS
+    return jnp.concatenate(
+        [jnp.broadcast_to(rows[o : o + 1], (share, WIDTH)) for o in range(OCTANTS)]
+    )
+
+
 def table_kernel(
     angles_far,
     three_far,
@@ -185,6 +192,7 @@
     need_three,
     need_four,
     fixed,
+    flags,
     sems,
 ):
     copies = [
@@ -203,7 +211,10 @@
     cones, boxes = need_three.shape
     fours = need_four.shape[1]
     copies[1].wait()
-    three_flags = flag_columns(need_three[...].astype(f32))
+    flags[...] = flag_columns(need_three[...].astype(f32))
+    three_flags = jnp.concatenate(
+        [flags[pl.ds(o, boxes // OCTANTS, stride=OCTANTS), :] for o in range(OCTANTS)]
+    )
     copies[2].wait()
     four_flags = flag_columns(need_four[...].astype(f32))
     for c in range(cones):
@@ -246,27 +257,33 @@
         c3, s3 = cosine_sine(dot(octants + 3 * OCTANTS, OCTANTS))
         column = jnp.broadcast_to(three_flags[:, c : c + 1], (boxes, WIDTH))
         at = pl.ds(c * boxes, boxes)
-        far_cos[at, :] = jnp.concatenate([c3] * (boxes // OCTANTS)) * column
-        far_sin[at, :] = jnp.concatenate([s3] * (boxes // OCTANTS)) * column
+        far_cos[at, :] = by_octant(c3, boxes) * column
+        far_sin[at, :] = by_octant(s3, boxes) * column
 
 
 def level_kernel(
-    gathered, high, low, far_cos, far_sin, keep, weights, out, lowfreq, turned
+    gathered, high, low, far_cos, far_sin, keep, weights, out, lowfreq
 ):
     boxes = gathered.shape[0] // OCTANTS
-    rows = keep.shape[0]
     half = OCTANTS // 2
-    start = pl.multiple_of(lax.axis_index(("half", "z", "y")) * OCTANTS, OCTANTS)
+    start = pl.multiple_of(lax.axis_index(("half", "y", "z")) * OCTANTS, OCTANTS)
     own = gathered[pl.ds(start, OCTANTS), :]
     even, odd = packed(own[:half], own[half:])
     for p in range(half):
         lowfreq[2 * p : 2 * p + 1, :] = even[p : p + 1]
         lowfreq[2 * p + 1 : 2 * p + 2, :] = odd[p : p + 1]
+    halves = 2
+    run = boxes // halves // OCTANTS
+
+    def octant_rows_of(row):
+        starts = [
+            (h * OCTANTS + o) * run * OCTANTS + row for o in range(OCTANTS) for h in range(halves)
+        ]
+        return jnp.concatenate([gathered[pl.ds(s, run, stride=OCTANTS), :] for s in starts])
+
     both = jnp.concatenate(
         [
-            jnp.concatenate(
-                [gathered[pl.ds(i * half + p, boxes, stride=OCTANTS), :] for p in range(half)], 1
-            )
+            jnp.concatenate([octant_rows_of(i * half + p) for p in range(half)], 1)
             for i in range(2)
         ]
     )
@@ -277,6 +294,7 @@
     )
     real = lax.broadcasted_iota(jnp.int32, (boxes, WIDTH), 1) < NODES
     sign = jnp.where(real, 1.0, -1.0)
+    cones = []
     for c in range(product.shape[1] // WIDTH):
         reals = product[:boxes, c * WIDTH : (c + 1) * WIDTH]
         imags = product[boxes:, c * WIDTH : (c + 1) * WIDTH]
@@ -284,9 +302,12 @@
         cosine = far_cos[at, :]
         sine = far_sin[at, :]
         across = (cosine * imags - sine * reals) * sign
-        turned[at, :] = (cosine * reals + sine * imags) + pltpu.roll(across, NODES, 1)
-    parts = [turned[pl.ds(o, rows, stride=OCTANTS), :] for o in range(OCTANTS)]
-    four = times(jnp.concatenate(parts, 1), weights[...])
+        turned = (cosine * reals + sine * imags) + pltpu.roll(across, NODES, 1)
+        share = boxes // OCTANTS
+        cones.append(
+            jnp.concatenate([turned[o * share : (o + 1) * share] for o in range(OCTANTS)], 1)
+        )
+    four = times(jnp.concatenate(cones), weights[...])
     out[...] = (four * keep[...]).reshape(out.shape)
 
 
@@ -350,6 +371,7 @@
             pltpu.VMEM(cone_need3.shape, jnp.int32),
             pltpu.VMEM(cone_need4.shape, jnp.int32),
             pltpu.VMEM(fixed.shape, f32),
+            pltpu.VMEM((boxes, width), f32),
             pltpu.SemaphoreType.DMA((4,)),
         ],
         compiler_params=pltpu.CompilerParams(vmem_limit_bytes=60 << 20),
@@ -363,7 +385,7 @@
     received, *tables = lax.optimization_barrier((received, *tables))
     gathered = lax.all_to_all(
         jnp.broadcast_to(received.sum(axis=0)[None], (blocks, 8, width)),
-        ("z", "y"),
+        ("y", "z"),
         split_axis=0,
         concat_axis=0,
         tiled=True,
@@ -377,7 +399,6 @@
         ],
         in_specs=[vmem()] * 7,
         out_specs=[vmem(), vmem()],
-        scratch_shapes=[pltpu.VMEM((cones * boxes, width), f32)],
         compiler_params=pltpu.CompilerParams(vmem_limit_bytes=24 << 20),
         name="levels",
     )(here(gathered), *[here(table) for table in tables], weights)

time: 48.1 us -> 48.2 us (level)
  no operation moved by 1% of the time
where the time goes in v6:
time: 48.2 us; the launch traced here: 47.9 us
  blocking collectives  34.1 us (71%)
  Pallas kernels  6.01 us (12%)
  starting transfers between devices  4.85 us (10%)
  waiting for transfers between devices  2.21 us (5%)
  between operations  0.65 us (1%)
    all_to_all x1, blocking collectives, local(): lax.all_to_all(jnp.broadcast_to(received.sum(axis=0)[None], (blocks, 8, w...  28.6 us
    all_gather x1, blocking collectives, local(): lax.all_gather(gathered.reshape(blocks * 8, width), 'half', tiled=True)  5.51 us
    all_to_all x1, starting transfers between devices, local(): lax.all_to_all(partial, 'sub', split_axis=0, concat_axis=0, tiled=True)  4.85 us
    all_to_all x1, waiting for transfers between devices, local(): lax.all_to_all(partial, 'sub', split_axis=0, concat_axis=0, tiled=True)  2.21 us
    pallas_call x1, Pallas kernels, local(): pl.pallas_call(leaf_kernel, out_shape=jax.ShapeDtypeStruct((subs, 8, widt...  2.15 us
    pallas_call x1, Pallas kernels, local(): pl.pallas_call(table_kernel, out_shape=[pltpu.VMEM((OCTANTS * NODES, cone...  1.99 us
    pallas_call x1, Pallas kernels, local(): pl.pallas_call(level_kernel, out_shape=[jax.ShapeDtypeStruct((cones, four...  1.87 us
  transfers between devices with their start and end apart: 1, of which 1 were waited for; matrix products, arithmetic and copies ran while one was open for 0% of the time, Pallas kernels for 4%

profile of v6, /device:TPU:1, one launch (start us, length us, event | category | flops | bytes accessed | tf_op | source)
XLA Modules:
  0.0 47.9 jit_solution(10143195800216981195)
XLA Ops:
  0.6 2.1 %leaves.1 = f32[4,8,128]{2,1,0:T(8,128)} custom-call(s32[4,128]{1,0:T(4,128)} %bitcast.3, bf16[512,128]{1,0:T(8,128)(2,1)} %constant.9.clone.narrow_far, f32[512,128]{1,0:T(8,128)} %leaves_far.1), custom_call_target="tpu_custom_call" | custom-call | tf_op jit(solution)/shard_map/leaves/pallas_call | solution.py:335
  2.8 4.9 %all-to-all-start = ((f32[4,8,128]{2,1,0:T(8,128)}), f32[4,8,128]{2,1,0:T(8,128)S(1)}, u32[]{:S(2)}, u32[]{:S(2)}) async-start(f32[4,8,128]{2,1,0:T(8,128)} %leaves.1), calls=%async_computation | async-start | bytes 32768 | tf_op jit(solution)/shard_map/all_to_all | solution.py:356
  7.6 2.0 %tables.1 = (bf16[512,768]{1,0:T(8,128)(2,1)S(1)}, bf16[512,768]{1,0:T(8,128)(2,1)S(1)}, f32[768,128]{1,0:T(8,128)S(1)}, f32[768,128]{1,0:T(8,128)S(1)}, f32[96,128]{1,0:T(8,128)S(1)}) custom-call(f32[2,768]{1,0:T(2,128)} %angles_far.1, s32[6,128]{1,0:T(8,128)} %three_far.1, s32[6,16]{1,0:T(8,128)} %four_far.1, f32[752,128]{1,0:T(8,128)} %constant.10.clone.fixed_far), custom_call_target="tpu_custom_call" | custom-call | tf_op jit(solution)/shard_map/tables/pallas_call | solution.py:358
  9.6 2.2 %all-to-all-done = f32[4,8,128]{2,1,0:T(8,128)S(1)} async-done(((f32[4,8,128]{2,1,0:T(8,128)}), f32[4,8,128]{2,1,0:T(8,128)S(1)}, u32[]{:S(2)}, u32[]{:S(2)}) %all-to-all-start) | async-done | bytes 16416 | tf_op jit(solution)/shard_map/all_to_all | solution.py:356
  11.9 28.6 %all_to_all.10 = f32[64,8,128]{2,1,0:T(8,128)S(1)} all-to-all(f32[64,8,128]{2,1,0:T(8,128)S(1)} %broadcast_in_dim.2), channel_id=1, replica_groups=mesh['half'=2,'z'=8,'y'=8,'sub'=4] {'y','z'}, dimensions={0} | all-to-all | bytes 524288 | tf_op jit(solution)/shard_map/all_to_all | solution.py:386
  40.5 0.0 copy-start
  40.5 5.5 %all_gather.3.gathered = f32[1024,128]{1,0:T(8,128)S(1)} all-gather(f32[512,128]{1,0:T(8,128)S(1)} %bitcast.2), channel_id=1, replica_groups=mesh['half'=2,'z'=8,'y'=8,'sub'=4] {'half'}, dimensions={0}, use_global_device_ids=true | all-gather | bytes 786432 | tf_op jit(solution)/shard_map/all_gather | solution.py:393
  46.0 0.0 copy-done
  46.0 1.9 %levels.1 = (f32[6,16,128]{2,1,0:T(8,128)}, f32[8,128]{1,0:T(8,128)}) custom-call(f32[1024,128]{1,0:T(8,128)S(1)} %all_gather.3.gathered, bf16[512,768]{1,0:T(8,128)(2,1)S(1)} %get-tuple-element.21.high, bf16[512,768]{1,0:T(8,128)(2,1)S(1)} %get-tuple-element.22.low, f32[768,128]{1,0:T(8,128)S(1)} %get-tuple-element.23.far_cos, ...), custom_call_target="tpu_custom_call" | custom-call | tf_op jit(solution)/shard_map/levels/pallas_call | solution.py:394
  (2 shorter events, 0.0 us)
Async XLA Ops:
  2.8 9.1 %all-to-all-start = ((f32[4,8,128]{2,1,0:T(8,128)}), f32[4,8,128]{2,1,0:T(8,128)S(1)}, u32[]{:S(2)}, u32[]{:S(2)}) async-start(f32[4,8,128]{2,1,0:T(8,128)} %leaves.1), calls=%async_computation | async-start | bytes 32768 | tf_op jit(solution)/shard_map/all_to_all | solution.py:356
  40.5 5.5 %copy-start = (bf16[1024,256]{1,0:T(8,128)(2,1)S(1)}, bf16[1024,256]{1,0:T(8,128)(2,1)}, u32[]{:S(2)}) copy-start(bf16[1024,256]{1,0:T(8,128)(2,1)} %constant.8.clone.weights) | copy-start | bytes 1572868
